TPU v7x, 32 devices: a whole 2x2x4 slice. The times are simulated.
32 devices in a mesh: exp: 8 (over y, x, core), tp: 4 (over z).
Axes of the slice: x: 2, y: 2, z: 4, core: 2. Of those that a mesh axis runs over, the one named last changes fastest.
Arguments:
- tokens: bfloat16 [65536, 384], P(('exp', 'tp')), may hold values from -24 to 24
- cotangent: bfloat16 [65536, 384], P(('exp', 'tp')), may hold values from -1 to 1
- routes: int32 [65536, 2], P(('exp', 'tp')), may hold values from 0 to 7, all different within a row; in each aligned block of 2048 rows (0 to 2047, 2048 to 4095, ...) at most 1024 rows name the same one
- segments: int32 [64, 1024], P(('exp', 'tp')), may hold values from 0 to 7, never falling along the last dimension, each value on 1 to 256 neighbouring positions
- variates: int32 [64, 1024], P(('exp', 'tp')), may hold values from 0 to 3
- positions: int32 [64, 1024], P(('exp', 'tp')), may hold values from 0 to 1023
- step_count: int32 [1], replicated, may hold values from 1 to 20
- dense_state: float32 [4, 592896], P(None, ('exp', 'tp')), as said below
- gate_up_state: float32 [4, 8, 2, 384, 512], P(None, 'exp', None, None, 'tp'), as said below
- down_state: float32 [4, 8, 512, 384], P(None, 'exp', 'tp'), as said below
- small_state: float32 [4, 780], replicated, as said below
Outputs:
- block_out: bfloat16 [65536, 384], P(('exp', 'tp'))
- grad_in: bfloat16 [65536, 384], P(('exp', 'tp'))
- dense_new: float32 [4, 592896], P(None, ('exp', 'tp'))
- dense_copy: bfloat16 [592896], P(('exp', 'tp'))
- gate_up_new: float32 [4, 8, 2, 384, 512], P(None, 'exp', None, None, 'tp')
- gate_up_copy: bfloat16 [8, 2, 384, 512], P('exp', None, None, 'tp')
- down_new: float32 [4, 8, 512, 384], P(None, 'exp', 'tp')
- down_copy: bfloat16 [8, 512, 384], P('exp', 'tp')
- small_new: float32 [4, 780], replicated
Inputs may be any that keep to these rules, and one draw needn't show every extreme that they name: `routes`: in each aligned block of 2048 rows (the tokens of one device) no expert is named by more than 1024 rows, a bound that some block reaches; the 2 ids of a row differ. `segments`: within a row the ids never fall; a segment has at most a quarter of 1024 tokens. `dense_state`: index 2 is positive. `gate_up_state`: index 2 is positive. `down_state`: index 2 is positive. `small_state`: index 2 is positive.
All inputs are finite; a program needn't handle non-finite values.
Results may differ from a plain program's by a relative error of at most 0.015.
Values may be sent and summed in bfloat16 or wider, within the bound.
No kernel may reach another device: no remote copies, remote signals or barrier semaphores. Data moves between devices by JAX's collectives and lax.ppermute only.
A program may use at most 384 MiB of HBM per device.

v0:
```python
from functools import partial
import math

import jax
import jax.numpy as jnp
from jax import lax
from jax.sharding import PartitionSpec as P

D = 384
HEADS = 6
HD = 64
TOP = 2
SEQ = 1024


norm_epsilon = 1e-06
masked_score = -1e30
moment_rate = 0.5
average_rate = 0.9
adam_epsilon = 1e-08
weight_decay = 0.1
rate_dense = 0.05
rate_expert = 0.04
rate_small = 0.2


def product(left, right):
    return jnp.dot(left, right, preferred_element_type=jnp.float32)


def left_product(left, right):
    return lax.dot_general(
        left, right, (((0,), (0,)), ((), ())), preferred_element_type=jnp.float32
    )


def right_product(left, right):
    return lax.dot_general(
        left, right, (((1,), (1,)), ((), ())), preferred_element_type=jnp.float32
    )


def normalize(values, gain):
    factor = lax.rsqrt(jnp.mean(values * values, axis=-1, keepdims=True) + norm_epsilon)
    return (values * factor * gain, factor)


def normalize_back(values, factor, gain, grad_out):
    weighted = grad_out * gain
    grad_gain = jnp.sum(grad_out * values * factor, axis=0)
    grad_values = factor * weighted - values * (factor * factor * factor) * jnp.mean(
        weighted * values, axis=-1, keepdims=True
    )
    return (grad_values, grad_gain)


def rotation(position_row):
    frequency = jnp.exp(jnp.arange(HD // 2, dtype=jnp.float32) * (-2.0 * math.log(10000.0) / HD))
    angles = position_row.astype(jnp.float32)[:, None] * frequency[None, :]
    return (jnp.cos(angles)[:, None, :], jnp.sin(angles)[:, None, :])


def rotate(values, cosine, sine_part, direction):
    half_dim = HD // 2
    front_half = values[..., :half_dim]
    back_half = values[..., half_dim:]
    return jnp.concatenate(
        [
            front_half * cosine - direction * back_half * sine_part,
            direction * front_half * sine_part + back_half * cosine,
        ],
        axis=-1,
    )


def make_masks(segment_row, variate_row):
    same_var = (variate_row[:, None] == variate_row[None, :])[None]
    allowed = (segment_row[:, None] == segment_row[None, :])[None]
    return (same_var, allowed)


def raw_scores(queries, key_rows, same_var, allowed, score_bias):
    scores = jnp.einsum(
        "qhd,khd->hqk", queries, key_rows, preferred_element_type=jnp.float32
    ) * HD ** (-0.5)
    scores = scores + jnp.where(
        same_var, score_bias[0][:, None, None], score_bias[1][:, None, None]
    )
    return jnp.where(allowed, scores, masked_score)


def attend_forward(score_bias, packed):
    queries, key_rows, values, segment_row, variate_row = packed
    same_var, allowed = make_masks(segment_row, variate_row)
    scores = raw_scores(queries, key_rows, same_var, allowed, score_bias)
    row_max = jnp.max(scores, axis=-1, keepdims=True)
    weights = jnp.exp(scores - row_max)
    row_total = jnp.sum(weights, axis=-1, keepdims=True)
    probs_low = (weights / row_total).astype(jnp.bfloat16)
    mixed_out = jnp.einsum("hqk,khd->qhd", probs_low, values, preferred_element_type=jnp.float32)
    return (mixed_out.astype(jnp.bfloat16), row_max + jnp.log(row_total))


def attend_backward(score_bias, packed):
    queries, key_rows, values, segment_row, variate_row, summary, grad_mixed = packed
    same_var, allowed = make_masks(segment_row, variate_row)
    probs_full = jnp.exp(raw_scores(queries, key_rows, same_var, allowed, score_bias) - summary)
    grad_probs = jnp.einsum("qhd,khd->hqk", grad_mixed, values, preferred_element_type=jnp.float32)
    grad_values = jnp.einsum(
        "hqk,qhd->khd",
        probs_full.astype(jnp.bfloat16),
        grad_mixed,
        preferred_element_type=jnp.float32,
    )
    row_inner = jnp.sum(probs_full * grad_probs, axis=-1, keepdims=True)
    grad_scores = (probs_full * (grad_probs - row_inner)).astype(jnp.bfloat16)
    score_grads = grad_scores.astype(jnp.float32)
    grad_bias = jnp.stack(
        [
            jnp.sum(jnp.where(same_var, score_grads, 0.0), axis=(1, 2)),
            jnp.sum(jnp.where(same_var, 0.0, score_grads), axis=(1, 2)),
        ]
    )
    grad_queries = jnp.einsum(
        "hqk,khd->qhd", grad_scores, key_rows, preferred_element_type=jnp.float32
    ) * HD ** (-0.5)
    grad_keys = jnp.einsum(
        "hqk,qhd->khd", grad_scores, queries, preferred_element_type=jnp.float32
    ) * HD ** (-0.5)
    return (grad_queries, grad_keys, grad_values, grad_bias)


def to_experts(outgoing):
    return lax.all_to_all(outgoing, "exp", split_axis=0, concat_axis=0, tiled=True)


def from_experts(results):
    return lax.all_to_all(results, "exp", split_axis=0, concat_axis=0, tiled=True)


def expert_forward(arrived, gate_up_low, down_low):
    gate_pre = product(arrived, gate_up_low[0, 0])
    up_pre = product(arrived, gate_up_low[0, 1])
    hidden = (jax.nn.silu(gate_pre) * up_pre).astype(jnp.bfloat16)
    results = product(hidden, down_low[0]).astype(jnp.bfloat16)
    return ((arrived, gate_pre, up_pre, hidden), results)


def expert_backward(stored, grad_arrived, gate_up_low, down_low):
    in_rows, gate_pre, up_pre, hidden = stored
    grad_hidden = right_product(grad_arrived, down_low[0])
    sigmoid = jax.nn.sigmoid(gate_pre)
    grad_gate = (grad_hidden * up_pre * sigmoid * (1.0 + gate_pre * (1.0 - sigmoid))).astype(
        jnp.bfloat16
    )
    grad_up = (grad_hidden * gate_pre * sigmoid).astype(jnp.bfloat16)
    grad_gate_up = jnp.stack([left_product(in_rows, grad_gate), left_product(in_rows, grad_up)])[
        None
    ]
    grad_down = left_product(hidden, grad_arrived)[None]
    grad_in_rows = (
        right_product(grad_gate, gate_up_low[0, 0]) + right_product(grad_up, gate_up_low[0, 1])
    ).astype(jnp.bfloat16)
    grad_gate_up, grad_down = (
        lax.psum_scatter(grad_gate_up, "tp", scatter_dimension=3, tiled=True),
        lax.psum_scatter(grad_down, "tp", scatter_dimension=1, tiled=True),
    )
    return (grad_in_rows, grad_gate_up, grad_down)


def adamw_update(old_state, grad_value, rate, decay, step_value):
    moment_one = moment_rate * old_state[1] + (1.0 - moment_rate) * grad_value
    moment_two = moment_rate * old_state[2] + (1.0 - moment_rate) * grad_value * grad_value
    correction = 1.0 - jnp.power(moment_rate, step_value)
    master = old_state[0] - rate * (
        moment_one / correction / (jnp.sqrt(moment_two / correction) + adam_epsilon)
        + decay * old_state[0]
    )
    average = average_rate * old_state[3] + (1.0 - average_rate) * master
    return jnp.stack([master, moment_one, moment_two, average])


def local(
    tokens,
    cotangent,
    routes,
    segments,
    variates,
    positions,
    step_count,
    dense_state,
    gate_up_state,
    down_state,
    small_state,
):
    tok_count = tokens.shape[0]
    seq_count = segments.shape[0]
    experts = lax.axis_size("exp") * gate_up_state.shape[1]
    capacity = 2 * tok_count * TOP // experts
    flat_weights = lax.all_gather(
        dense_state[0].astype(jnp.bfloat16), ("exp", "tp"), axis=0, tiled=True
    )
    in_proj = flat_weights[: 3 * D * D].reshape(D, 3 * D)
    out_proj = flat_weights[3 * D * D : 4 * D * D].reshape(D, D)
    router_weight = flat_weights[4 * D * D :].reshape(D, experts)
    small_params = small_state[0]
    gain_one = small_params[:D]
    gain_two = small_params[D : 2 * D]
    score_bias = small_params[2 * D :].reshape(2, HEADS)
    gate_up_low = gate_up_state[0].astype(jnp.bfloat16)
    down_low = down_state[0].astype(jnp.bfloat16)
    gate_up_low, down_low = (
        lax.all_gather(gate_up_low, "tp", axis=3, tiled=True),
        lax.all_gather(down_low, "tp", axis=1, tiled=True),
    )
    inputs = tokens.astype(jnp.float32)
    normed_one, scale_one = normalize(inputs, gain_one)
    normed_one = normed_one.astype(jnp.bfloat16)
    projected = product(normed_one, in_proj)
    cosine, sine_part = rotation(positions.reshape(-1))
    queries = rotate(projected[:, :D].reshape(tok_count, HEADS, HD), cosine, sine_part, 1.0).astype(
        jnp.bfloat16
    )
    key_rows = rotate(
        projected[:, D : 2 * D].reshape(tok_count, HEADS, HD), cosine, sine_part, 1.0
    ).astype(jnp.bfloat16)
    values = projected[:, 2 * D :].reshape(tok_count, HEADS, HD).astype(jnp.bfloat16)
    seq_queries = queries.reshape(seq_count, SEQ, HEADS, HD)
    seq_keys = key_rows.reshape(seq_count, SEQ, HEADS, HD)
    seq_values = values.reshape(seq_count, SEQ, HEADS, HD)
    mixed_out, summary = lax.map(
        partial(attend_forward, score_bias), (seq_queries, seq_keys, seq_values, segments, variates)
    )
    mixed_out = mixed_out.reshape(tok_count, D)
    middle = inputs + product(mixed_out, out_proj)
    normed_two, scale_two = normalize(middle, gain_two)
    normed_two = normed_two.astype(jnp.bfloat16)
    logits = product(normed_two, router_weight)
    select = routes[:, :, None] == jnp.arange(experts, dtype=jnp.int32)[None, None, :]
    chosen = jnp.sum(jnp.where(select, logits[:, None, :], 0.0), axis=-1)
    gate_probs = jax.nn.softmax(chosen, axis=-1)
    pair_routes = routes.reshape(-1)
    matches = (pair_routes[:, None] == jnp.arange(experts, dtype=jnp.int32)[None, :]).astype(
        jnp.int32
    )
    slot_rank = jnp.sum((jnp.cumsum(matches, axis=0) - matches) * matches, axis=1)
    slot_index = pair_routes * capacity + slot_rank
    source = (
        jnp.zeros((experts * capacity,), jnp.int32)
        .at[slot_index]
        .set(jnp.arange(tok_count * TOP, dtype=jnp.int32))
    )
    filled = jnp.zeros((experts * capacity,), jnp.int32).at[slot_index].set(1) > 0
    outgoing = jnp.where(filled[:, None], normed_two[source // TOP], 0)
    cot_values = cotangent.astype(jnp.float32)
    grad_pairs = (
        (gate_probs[:, :, None] * cot_values[:, None, :])
        .reshape(tok_count * TOP, D)
        .astype(jnp.bfloat16)
    )
    grad_outgoing = jnp.where(filled[:, None], grad_pairs[source], 0)
    arrived = to_experts(outgoing)
    stored, results = expert_forward(arrived, gate_up_low, down_low)
    returned = from_experts(results)
    grad_arrived = to_experts(grad_outgoing)
    grad_rows, grad_gate_up, grad_down = expert_backward(
        stored, grad_arrived, gate_up_low, down_low
    )
    grad_returned = from_experts(grad_rows)
    out_pairs = returned[slot_index].astype(jnp.float32).reshape(tok_count, TOP, D)
    block_out = (middle + jnp.sum(gate_probs[:, :, None] * out_pairs, axis=1)).astype(jnp.bfloat16)
    grad_gate = jnp.sum(cot_values[:, None, :] * out_pairs, axis=-1)
    grad_chosen = gate_probs * (grad_gate - jnp.sum(gate_probs * grad_gate, axis=-1, keepdims=True))
    grad_logits = jnp.sum(jnp.where(select, grad_chosen[:, :, None], 0.0), axis=1).astype(
        jnp.bfloat16
    )
    back_pairs = grad_returned[slot_index].astype(jnp.float32).reshape(tok_count, TOP, D)
    grad_normed_two = right_product(grad_logits, router_weight) + jnp.sum(back_pairs, axis=1)
    grad_router = left_product(normed_two, grad_logits)
    grad_middle, grad_gain_two = normalize_back(middle, scale_two, gain_two, grad_normed_two)
    grad_middle = grad_middle + cot_values
    grad_branch = grad_middle.astype(jnp.bfloat16)
    grad_out_proj = left_product(mixed_out, grad_branch)
    grad_mixed = (
        right_product(grad_branch, out_proj).astype(jnp.bfloat16).reshape(seq_count, SEQ, HEADS, HD)
    )
    grad_queries, grad_keys, grad_values, grad_bias = lax.map(
        partial(attend_backward, score_bias),
        (seq_queries, seq_keys, seq_values, segments, variates, summary, grad_mixed),
    )
    grad_bias = jnp.sum(grad_bias, axis=0)
    grad_queries = rotate(
        grad_queries.reshape(tok_count, HEADS, HD), cosine, sine_part, -1.0
    ).reshape(tok_count, D)
    grad_keys = rotate(grad_keys.reshape(tok_count, HEADS, HD), cosine, sine_part, -1.0).reshape(
        tok_count, D
    )
    grad_projected = jnp.concatenate(
        [grad_queries, grad_keys, grad_values.reshape(tok_count, D)], axis=1
    ).astype(jnp.bfloat16)
    grad_in_proj = left_product(normed_one, grad_projected)
    grad_normed_one = right_product(grad_projected, in_proj)
    grad_inputs, grad_gain_one = normalize_back(inputs, scale_one, gain_one, grad_normed_one)
    grad_in = (grad_middle + grad_inputs).astype(jnp.bfloat16)
    dense_grad = jnp.concatenate(
        [grad_in_proj.reshape(-1), grad_out_proj.reshape(-1), grad_router.reshape(-1)]
    )
    dense_grad = lax.psum_scatter(dense_grad, ("exp", "tp"), scatter_dimension=0, tiled=True)
    small_grad = lax.psum(
        jnp.concatenate([grad_gain_one, grad_gain_two, grad_bias.reshape(-1)]), ("exp", "tp")
    )
    step_value = step_count[0].astype(jnp.float32)
    dense_new = adamw_update(dense_state, dense_grad, rate_dense, weight_decay, step_value)
    gate_up_new = adamw_update(gate_up_state, grad_gate_up, rate_expert, weight_decay, step_value)
    down_new = adamw_update(down_state, grad_down, rate_expert, weight_decay, step_value)
    small_new = adamw_update(small_state, small_grad, rate_small, 0.0, step_value)
    return (
        block_out,
        grad_in,
        dense_new,
        dense_new[0].astype(jnp.bfloat16),
        gate_up_new,
        gate_up_new[0].astype(jnp.bfloat16),
        down_new,
        down_new[0].astype(jnp.bfloat16),
        small_new,
    )


def solution(mesh):
    in_specs = (
        P(("exp", "tp"), None),
        P(("exp", "tp"), None),
        P(("exp", "tp"), None),
        P(("exp", "tp"), None),
        P(("exp", "tp"), None),
        P(("exp", "tp"), None),
        P(),
        P(None, ("exp", "tp")),
        P(None, "exp", None, None, "tp"),
        P(None, "exp", "tp", None),
        P(),
    )
    out_specs = (
        P(("exp", "tp"), None),
        P(("exp", "tp"), None),
        P(None, ("exp", "tp")),
        P(("exp", "tp")),
        P(None, "exp", None, None, "tp"),
        P("exp", None, None, "tp"),
        P(None, "exp", "tp", None),
        P("exp", "tp", None),
        P(),
    )
    return jax.shard_map(local, mesh=mesh, in_specs=in_specs, out_specs=out_specs, check_vma=False)
```

profile of v0, /device:TPU:0, one launch (start us, length us, event | category | flops | bytes accessed | tf_op | source)
XLA Modules:
  0.0 1325.2 jit_solution(2155927653004741738)
XLA Ops:
  19.1 15.5 %scatter_custom_fusion.1 = s32[8192]{0:T(1024)S(1)} fusion(s32[4096]{0:T(1024)S(1)} %bitcast.346, s32[4096]{0:T(1024)S(1)} %iota.21, s32[]{:T(128)} %constant.51.clone.1), kind=kCustom, calls=%fused_computation.210 | custom fusion | bytes 32772 | tf_op jit(solution)/shard_map/scatter | solution.py:251
  34.6 15.8 %scatter_custom_fusion = s32[8192]{0:T(1024)S(1)} fusion(s32[4096]{0:T(1024)S(1)} %bitcast.347, s32[4096]{0:T(1024)S(1)} %broadcast.453, s32[]{:T(128)} %constant.51.clone.1), kind=kCustom, calls=%fused_computation.213 | custom fusion | bytes 32772 | tf_op jit(solution)/shard_map/scatter | solution.py:253
  57.5 6.7 mul.671
  64.3 8.5 mul.676
  76.0 70.9 %all-reduce.5.cloned.1.call-done = bf16[592896]{0:T(1024)(128)(2,1)} async-done(((bf16[592896]{0:T(1024)(128)(2,1)}), bf16[592896]{0:T(1024)(128)(2,1)}) %all-reduce.5.cloned.1.call-update) | async-done | bytes 1185808
  159.7 4.6 subtract_convert_fusion.2
  182.2 85.0 %while.28 = (s32[]{:T(128)}, bf16[2,1024,6,64]{1,3,2,0:T(8,128)(2,1)}, f32[2,6,1024,1]{2,1,3,0:T(8,128)S(1)}, bf16[2,1024,6,64]{1,3,2,0:T(8,128)(2,1)}, s32[2,10...) while((s32[]{:T(128)}, ...), condition=%wide.region_4.5_spmd, body=%wide.region_1.4_spmd.sunk | while | flops 1726343168 | bytes 106172760 | solution.py:231
  184.1 13.3 %fusion.149 = (f32[6,1024]{1,0:T(8,128)S(1)}, f32[6,1024,1024]{1,2,0:T(8,128)}) fusion(f32[6]{0:T(128)S(1)} %get-tuple-element.555, f32[6]{0:T(128)S(1)} %get-tuple-element.556, pred[1024,1024]{0,1:T(8,128)(4,1)S(1)} %broadcast_compare_fusion.9, pred[1024,1024]{0,1:T(8,128)(4,1)S(1)} %broadcast_compare_fusion.10, ...), kind=kOutput, calls=%fused_computation.10.clone.1 | convolution fusion | flops 836757504 | bytes 28862464 | tf_op jit(solution)/shard_map/while/body/eval_jaxpr/qhd,khd->hqk/dot_general | solution.py:83
  197.4 12.6 fusion.150
  210.0 13.7 %fusion.151 = bf16[2,1024,6,64]{1,3,2,0:T(8,128)(2,1)S(1)} fusion(bf16[2,1024,6,64]{1,3,2,0:T(8,128)(2,1)S(1)} %copy-done.31, s32[]{:T(128)S(6)} %copy.217, f32[6,1024,1024]{1,2,0:T(8,128)} %get-tuple-element.559, f32[6,1024]{1,0:T(8,128)S(1)} %fusion.150, f32[6,1024]{1,0:T(8,128)S(1)} %get-tuple-element.560, f32[6]{0:T(128)S(1)} %get-tuple-element.555, ...), kind=kOutput, calls=%fused_computation.16.clone.1 | convolution fusion | flops 849739776 | bytes 28903424 | tf_op jit(solution)/shard_map/while/body/eval_jaxpr/hqk,khd->qhd/dot_general | solution.py:100
  226.3 13.3 %fusion.149 = (f32[6,1024]{1,0:T(8,128)S(1)}, f32[6,1024,1024]{1,2,0:T(8,128)}) fusion(f32[6]{0:T(128)S(1)} %get-tuple-element.555, f32[6]{0:T(128)S(1)} %get-tuple-element.556, pred[1024,1024]{0,1:T(8,128)(4,1)S(1)} %broadcast_compare_fusion.9, pred[1024,1024]{0,1:T(8,128)(4,1)S(1)} %broadcast_compare_fusion.10, ...), kind=kOutput, calls=%fused_computation.10.clone.1 | convolution fusion | flops 836757504 | bytes 28862464 | tf_op jit(solution)/shard_map/while/body/eval_jaxpr/qhd,khd->hqk/dot_general | solution.py:83
  239.6 12.6 fusion.150
  252.2 13.7 %fusion.151 = bf16[2,1024,6,64]{1,3,2,0:T(8,128)(2,1)S(1)} fusion(bf16[2,1024,6,64]{1,3,2,0:T(8,128)(2,1)S(1)} %copy-done.31, s32[]{:T(128)S(6)} %copy.217, f32[6,1024,1024]{1,2,0:T(8,128)} %get-tuple-element.559, f32[6,1024]{1,0:T(8,128)S(1)} %fusion.150, f32[6,1024]{1,0:T(8,128)S(1)} %get-tuple-element.560, f32[6]{0:T(128)S(1)} %get-tuple-element.555, ...), kind=kOutput, calls=%fused_computation.16.clone.1 | convolution fusion | flops 849739776 | bytes 28903424 | tf_op jit(solution)/shard_map/while/body/eval_jaxpr/hqk,khd->qhd/dot_general | solution.py:100
  267.3 4.2 copy.143
  280.3 4.4 multiply_convert_fusion.4
  284.8 34.8 %gather_fusion.2 = bf16[8192,384]{1,0:T(8,128)(2,1)} fusion(bf16[4096,384]{1,0:T(8,128)(2,1)} %multiply_convert_fusion.4, s32[8192]{0:T(1024)S(1)} %copy-done.59), kind=kCustom, calls=%fused_computation.2 | custom fusion | bytes 12615680 | tf_op jit(solution)/shard_map/gather | solution.py:261
  319.5 33.1 %gather_fusion = bf16[8192,384]{1,0:T(8,128)(2,1)} fusion(bf16[2048,384]{1,0:T(8,128)(2,1)S(1)} %copy.148, s32[8192]{0:T(1024)S(1)} %copy-done.58), kind=kCustom, calls=%fused_computation | custom fusion | bytes 12615680 | tf_op jit(solution)/shard_map/gather | solution.py:254
  352.7 9.0 broadcast_select_fusion
  361.6 74.9 %all_to_all.42 = bf16[8,1024,384]{2,1,0:T(8,128)(2,1)} all-to-all(bf16[8,1024,384]{2,1,0:T(8,128)(2,1)S(1)} %get-tuple-element.412), channel_id=1, replica_groups=mesh['exp'=8,'tp'=4] {'exp'}, dimensions={0} | all-to-all | bytes 12582912 | tf_op jit(solution)/shard_map/all_to_all | solution.py:134
  436.5 4.8 all-to-all-start.2
  442.2 15.1 %all_gather.11 = bf16[1,512,384]{2,1,0:T(8,128)(2,1)S(1)} all-gather(bf16[1,128,384]{2,1,0:T(8,128)(2,1)S(1)} %bitcast_convert_fusion.1), channel_id=1, replica_groups=mesh['exp'=8,'tp'=4] {'tp'}, dimensions={1}, use_global_device_ids=true | all-gather | bytes 491520 | tf_op jit(solution)/shard_map/all_gather | solution.py:214
  458.4 18.0 %all_gather.10 = bf16[1,2,384,512]{3,2,1,0:T(8,128)(2,1)S(1)} all-gather(bf16[1,2,384,128]{3,2,1,0:T(8,128)(2,1)S(1)} %bitcast_convert_fusion), channel_id=1, replica_groups=mesh['exp'=8,'tp'=4] {'tp'}, dimensions={3}, use_global_device_ids=true | all-gather | bytes 983040 | tf_op jit(solution)/shard_map/all_gather | solution.py:213
  476.4 11.7 fusion.70
  488.0 8.1 fusion.69
  496.1 16.8 %all-to-all-done.2 = bf16[8,1024,384]{2,1,0:T(8,128)(2,1)} async-done(((bf16[8,1024,384]{2,1,0:T(8,128)(2,1)}), bf16[8,1024,384]{2,1,0:T(8,128)(2,1)}, u32[]{:S(2)}, u32[]{:S(2)}) %all-to-all-start.2) | async-done | bytes 6291488 | tf_op jit(solution)/shard_map/all_to_all | solution.py:134
  512.9 26.0 %multiply_convert_fusion.1 = (bf16[8192,512]{1,0:T(8,128)(2,1)}, bf16[8192,512]{1,0:T(8,128)(2,1)}, bf16[8192,512]{1,0:T(8,128)(2,1)}) fusion(f32[8192,512]{1,0:T(8,128)} %fusion.69, f32[8192,512]{1,0:T(8,128)} %fusion.70, bf16[8192,384]{1,0:T(8,128)(2,1)} %bitcast.43, bf16[1,512,384]{2,1,0:T(8,128)(2,1)S(1)} %all_gather.11), kind=kOutput, calls=%fused_computation.74 | convolution fusion | flops 3288334336 | bytes 65404928 | tf_op jit(solution)/shard_map/dot_general | solution.py:38
  538.9 7.5 fusion.68
  546.4 10.5 add_convert_fusion
  556.9 4.8 all-to-all-start.3
  561.7 10.6 convolution_bitcast_fusion
  572.3 10.6 convolution_convert_fusion
  582.9 50.4 %all-to-all-done.3 = bf16[8,1024,384]{2,1,0:T(8,128)(2,1)} async-done(((bf16[8,1024,384]{2,1,0:T(8,128)(2,1)}), bf16[8,1024,384]{2,1,0:T(8,128)(2,1)}, u32[]{:S(2)}, u32[]{:S(2)}) %all-to-all-start.3) | async-done | bytes 6291488 | tf_op jit(solution)/shard_map/all_to_all | solution.py:138
  633.3 5.0 all-to-all-start.1
  638.3 7.8 convolution_bitcast_fusion.1
  646.1 7.8 convolution_bitcast_fusion.2
  659.6 32.7 %reduce-scatter.3.cloned.1.call-done = f32[1,2,384,128]{3,2,1,0:T(8,128)} async-done(((f32[1,2,384,512]{3,2,1,0:T(8,128)}), f32[1,2,384,128]{3,2,1,0:T(8,128)}) %reduce-scatter.3.cloned.1.call-update) | async-done | bytes 393232 | tf_op jit(solution)/shard_map/reduce_scatter | solution.py:165
  695.5 17.6 %gather_fusion.3 = bf16[4096,384]{1,0:T(8,128)(2,1)S(1)} fusion(bf16[8192,384]{1,0:T(8,128)(2,1)} %bitcast.45, s32[4096]{0:T(1024)S(1)} %broadcast_clamp_fusion), kind=kCustom, calls=%fused_computation.3 | custom fusion | bytes 6307840 | tf_op jit(solution)/shard_map/gather | solution.py:277
  713.2 4.8 reshape.700
  717.9 27.3 %reduce_sum.183 = f32[2048,384]{1,0:T(8,128)S(1)} reduce(f32[2048,2,384]{2,1,0:T(2,128)} %reshape.700, f32[]{:T(128)} %constant.55.clone.1), dimensions={1}, to_apply=%region_18.19 | reduce | flops 786432 | bytes 9437188 | tf_op jit(solution)/shard_map/reduce_sum | solution.py:278
  747.7 17.6 %gather_fusion.1 = bf16[4096,384]{1,0:T(8,128)(2,1)S(1)} fusion(bf16[8192,384]{1,0:T(8,128)(2,1)} %bitcast.41, s32[4096]{0:T(1024)S(1)} %broadcast_clamp_fusion), kind=kCustom, calls=%fused_computation.1 | custom fusion | bytes 6307840 | tf_op jit(solution)/shard_map/gather | solution.py:270
  765.3 4.7 reshape.699
  770.0 19.8 %multiply_reduce_fusion.1 = (f32[2048,2]{1,0:T(8,128)}, f32[2048,384]{1,0:T(8,128)}) fusion(f32[2048,2,384]{2,1,0:T(2,128)} %reshape.699, f32[2048,384]{1,0:T(8,128)} %copy.151, f32[2048,2]{1,0:T(8,128)} %copy.144), kind=kLoop, calls=%fused_computation.87 | loop fusion | flops 5500928 | bytes 12615680 | tf_op jit(solution)/shard_map/reduce_sum | solution.py:272
  794.2 5.1 multiply_reduce_fusion.3
  802.8 6.0 subtract_add_fusion
  815.5 290.6 %while.29 = (s32[]{:T(128)}, f32[2,1024,6,64]{1,0,3,2:T(2,128)}, f32[2,1024,6,64]{1,0,3,2:T(2,128)}, bf16[2,1024,6,64]{1,3,2,0:T(8,128)(2,1)}, f32[2,2,6]{2,1,0:...) while((s32[]{:T(128)}, f32[2,1024,6,64]{1,0,3,2:T(2,128)}, ...), condition=%wide.region_24.25_spmd, body=%wide.region_20.24_spmd.sunk | while | flops 4130072576 | bytes 286152160 | solution.py:287
  817.1 13.1 fusion.160
  830.2 20.6 %multiply_reduce_fusion.14 = (f32[6,1024]{1,0:T(8,128)S(1)}, f32[6,1024,1024]{1,2,0:T(8,128)}) fusion(f32[6,1024,1024]{1,2,0:T(8,128)} %fusion.160, f32[6,1024]{1,0:T(8,128)S(1)} %dynamic-slice_bitcast_fusion.2, f32[6]{0:T(128)S(1)} %get-tuple-element.575, f32[6]{0:T(128)S(1)} %get-tuple-element.576, ...), kind=kOutput, calls=%fused_computation.38.clone.1 | convolution fusion | flops 849340416 | bytes 54051888 | tf_op jit(solution)/shard_map/while/body/eval_jaxpr/qhd,khd->hqk/dot_general | solution.py:83
  850.8 23.3 %fusion.161 = (f32[6]{0:T(128)S(1)}, f32[6]{0:T(128)S(1)}, bf16[6,1024,1024]{1,2,0:T(8,128)(2,1)}) fusion(pred[1024,1024]{0,1:T(8,128)(4,1)S(1)} %broadcast_compare_fusion.11, f32[6,1024,1024]{1,2,0:T(8,128)} %get-tuple-element.578, f32[6,1024,1024]{1,2,0:T(8,128)} %fusion.160, f32[6,1024]{1,0:T(8,128)S(1)} %get-tuple-element.579), kind=kLoop, calls=%fused_computation.35.clone.1 | loop fusion | flops 50331632 | bytes 63987760 | tf_op jit(solution)/shard_map/while/body/eval_jaxpr/reduce_sum | solution.py:120
  874.1 12.3 bitcast_dynamic-update-slice_fusion.5
  887.6 8.9 multiply_bitcast_fusion.5
  905.5 27.8 %dynamic_update_slice.37 = f32[2,1024,6,64]{1,0,3,2:T(2,128)} dynamic-update-slice(f32[2,1024,6,64]{1,0,3,2:T(2,128)} %get-tuple-element.630, f32[1,1024,6,64]{1,0,3,2:T(1,128)} %copy.205, s32[]{:T(128)S(6)} %copy.228, s32[]{:T(128)} %constant.51.clone.1..sunk, s32[]{:T(128)} %constant.51.clone.1..sunk, s32[]{:T(128)} %constant.51.clone.1..sunk) | dynamic-update-slice | bytes 3145732 | tf_op jit(solution)/shard_map/while/body/jit(dynamic_update_index_in_dim)/dynamic_update_slice | solution.py:287
  933.3 27.5 %dynamic_update_slice.36 = f32[2,1024,6,64]{1,0,3,2:T(2,128)} dynamic-update-slice(f32[2,1024,6,64]{1,0,3,2:T(2,128)} %get-tuple-element.629, f32[1,1024,6,64]{1,0,3,2:T(1,128)S(1)} %copy-done.1, s32[]{:T(128)S(6)} %copy.228, s32[]{:T(128)} %constant.51.clone.1..sunk, s32[]{:T(128)} %constant.51.clone.1..sunk, s32[]{:T(128)} %constant.51.clone.1..sunk) | dynamic-update-slice | bytes 3145732 | tf_op jit(solution)/shard_map/while/body/jit(dynamic_update_index_in_dim)/dynamic_update_slice | solution.py:287
  962.2 13.1 fusion.160
  975.3 20.6 %multiply_reduce_fusion.14 = (f32[6,1024]{1,0:T(8,128)S(1)}, f32[6,1024,1024]{1,2,0:T(8,128)}) fusion(f32[6,1024,1024]{1,2,0:T(8,128)} %fusion.160, f32[6,1024]{1,0:T(8,128)S(1)} %dynamic-slice_bitcast_fusion.2, f32[6]{0:T(128)S(1)} %get-tuple-element.575, f32[6]{0:T(128)S(1)} %get-tuple-element.576, ...), kind=kOutput, calls=%fused_computation.38.clone.1 | convolution fusion | flops 849340416 | bytes 54051888 | tf_op jit(solution)/shard_map/while/body/eval_jaxpr/qhd,khd->hqk/dot_general | solution.py:83
  995.9 23.3 %fusion.161 = (f32[6]{0:T(128)S(1)}, f32[6]{0:T(128)S(1)}, bf16[6,1024,1024]{1,2,0:T(8,128)(2,1)}) fusion(pred[1024,1024]{0,1:T(8,128)(4,1)S(1)} %broadcast_compare_fusion.11, f32[6,1024,1024]{1,2,0:T(8,128)} %get-tuple-element.578, f32[6,1024,1024]{1,2,0:T(8,128)} %fusion.160, f32[6,1024]{1,0:T(8,128)S(1)} %get-tuple-element.579), kind=kLoop, calls=%fused_computation.35.clone.1 | loop fusion | flops 50331632 | bytes 63987760 | tf_op jit(solution)/shard_map/while/body/eval_jaxpr/reduce_sum | solution.py:120
  1019.2 12.3 bitcast_dynamic-update-slice_fusion.5
  1032.7 8.9 multiply_bitcast_fusion.5
  1050.6 27.8 %dynamic_update_slice.37 = f32[2,1024,6,64]{1,0,3,2:T(2,128)} dynamic-update-slice(f32[2,1024,6,64]{1,0,3,2:T(2,128)} %get-tuple-element.630, f32[1,1024,6,64]{1,0,3,2:T(1,128)} %copy.205, s32[]{:T(128)S(6)} %copy.228, s32[]{:T(128)} %constant.51.clone.1..sunk, s32[]{:T(128)} %constant.51.clone.1..sunk, s32[]{:T(128)} %constant.51.clone.1..sunk) | dynamic-update-slice | bytes 3145732 | tf_op jit(solution)/shard_map/while/body/jit(dynamic_update_index_in_dim)/dynamic_update_slice | solution.py:287
  1078.4 27.5 %dynamic_update_slice.36 = f32[2,1024,6,64]{1,0,3,2:T(2,128)} dynamic-update-slice(f32[2,1024,6,64]{1,0,3,2:T(2,128)} %get-tuple-element.629, f32[1,1024,6,64]{1,0,3,2:T(1,128)S(1)} %copy-done.1, s32[]{:T(128)S(6)} %copy.228, s32[]{:T(128)} %constant.51.clone.1..sunk, s32[]{:T(128)} %constant.51.clone.1..sunk, s32[]{:T(128)} %constant.51.clone.1..sunk) | dynamic-update-slice | bytes 3145732 | tf_op jit(solution)/shard_map/while/body/jit(dynamic_update_index_in_dim)/dynamic_update_slice | solution.py:287
  1110.7 4.3 reshape.690
  1115.0 5.7 reshape.692
  1129.0 4.1 fusion.52
  1136.9 39.5 %psum.7 = f32[780]{0:T(1024)S(1)} all-reduce(f32[780]{0:T(1024)S(1)} %pad_maximum_fusion.12), channel_id=1, replica_groups=mesh['exp'=8,'tp'=4] {'exp','tp'}, use_global_device_ids=true, to_apply=%region_32.33 | all-reduce | flops 780 | bytes 6240 | tf_op jit(solution)/shard_map/psum | solution.py:309
  1186.8 128.5 %all-reduce.7.cloned.1.call-done = f32[592896]{0:T(1024)} async-done(((f32[592896]{0:T(1024)}), f32[592896]{0:T(1024)}) %all-reduce.7.cloned.1.call-update) | async-done | bytes 2371600
  (346 shorter events, 146.0 us)
Async XLA Ops:
  7.2 5.7 copy-start.46
  7.2 139.7 %all-reduce.5.cloned.1.call-start = ((), (), s32[]{:S(2)}) async-start(), calls=%async_computation.8 | async-start | bytes 2371584
  7.2 7.7 copy-start.81
  12.9 38.2 %copy-start.28 = (bf16[2048,384]{1,0:T(8,128)(2,1)S(1)}, bf16[2048,384]{1,0:T(8,128)(2,1)}, u32[]{:S(2)}) copy-start(bf16[2048,384]{1,0:T(8,128)(2,1)} %param.15) | copy-start | bytes 4718596
  19.0 31.4 %copy-start.66 = (s32[4096,1]{0,1:T(1,128)}, s32[4096,1]{0,1:T(1,128)S(1)}, u32[]{:S(2)}) copy-start(s32[4096,1]{0,1:T(1,128)S(1)} %compare_select_fusion) | copy-start | bytes 49156
  51.8 97.3 %copy-start.4 = (bf16[2048,384]{0,1:T(8,128)(2,1)}, bf16[2048,384]{0,1:T(8,128)(2,1)S(1)}, u32[]{:S(2)}) copy-start(bf16[2048,384]{0,1:T(8,128)(2,1)S(1)} %copy.139) | copy-start | bytes 4718596
  53.0 96.2 %copy-start.56 = (f32[2048]{0:T(1024)}, f32[2048]{0:T(1024)S(1)}, u32[]{:S(2)}) copy-start(f32[2048]{0:T(1024)S(1)} %get-tuple-element.408) | copy-start | bytes 24580
  55.4 8.9 copy-start.13
  74.1 77.8 %copy-start.68 = (f32[384]{0:T(512)}, f32[384]{0:T(512)S(1)}, u32[]{:S(2)}) copy-start(f32[384]{0:T(512)S(1)} %get-tuple-element.305) | copy-start | bytes 4612
  153.3 6.4 copy-start.25
  167.5 4.7 copy-start.22
  172.8 3.7 copy-start.21
  178.6 3.7 copy-start.51
  178.6 3.7 copy-start.53
  197.4 12.6 copy-start.12
  197.4 12.6 copy-start.31
  239.6 12.6 copy-start.12
  239.6 12.6 copy-start.31
  267.2 4.7 copy-start.10
  267.3 4.7 copy-start.11
  267.3 4.7 copy-start.41
  267.3 4.7 copy-start.64
  267.3 4.7 copy-start.5
  267.3 4.7 copy-start.23
  275.2 5.1 copy-start.14
  276.5 8.2 copy-start.39
  276.6 8.2 copy-start.49
  280.3 4.5 copy-start.59
  284.8 34.8 %copy-start.58 = (s32[8192]{0:T(1024)S(1)}, s32[8192]{0:T(1024)}, u32[]{:S(2)}) copy-start(s32[8192]{0:T(1024)} %get-tuple-element.403) | copy-start | bytes 98308
  319.5 33.1 %copy-start.74 = (pred[8,1024]{1,0:T(8,128)(4,1)S(1)}, pred[8,1024]{1,0:T(8,128)(4,1)}, u32[]{:S(2)}) copy-start(pred[8,1024]{1,0:T(8,128)(4,1)} %broadcast_in_dim.212) | copy-start | bytes 24580
  436.5 76.4 %all-to-all-start.2 = ((bf16[8,1024,384]{2,1,0:T(8,128)(2,1)}), bf16[8,1024,384]{2,1,0:T(8,128)(2,1)}, u32[]{:S(2)}, u32[]{:S(2)}) async-start(bf16[8,1024,384]{2,1,0:T(8,128)(2,1)} %get-tuple-element.411), calls=%async_computation.2 | async-start | bytes 12582912 | tf_op jit(solution)/shard_map/all_to_all | solution.py:134
  458.3 29.7 %slice-start = ((s8[6291456]{0:T(1024)(128)(4,1)}), s8[4194304]{0:T(1024)(128)(4,1)S(1)}, s32[]{:S(2)}) async-start(s8[6291456]{0:T(1024)(128)(4,1)} %bitcast.320), calls=%async_computation.10 | async-start | bytes 8388608
  476.3 11.7 copy-start.15
  476.4 11.7 slice-start.1
  556.9 76.4 %all-to-all-start.3 = ((bf16[8,1024,384]{2,1,0:T(8,128)(2,1)}), bf16[8,1024,384]{2,1,0:T(8,128)(2,1)}, u32[]{:S(2)}, u32[]{:S(2)}) async-start(bf16[8,1024,384]{2,1,0:T(8,128)(2,1)} %bitcast.323), calls=%async_computation.3 | async-start | bytes 12582912 | tf_op jit(solution)/shard_map/all_to_all | solution.py:138
  561.7 95.2 %reduce-scatter.5.cloned.1.call-start = ((), (), s32[]{:S(2)}) async-start(), calls=%async_computation.7 | async-start | bytes 983040 | tf_op jit(solution)/shard_map/reduce_scatter | solution.py:166
  633.3 114.4 %all-to-all-start.1 = ((bf16[8,1024,384]{2,1,0:T(8,128)(2,1)}), bf16[8,1024,384]{2,1,0:T(8,128)(2,1)}, u32[]{:S(2)}, u32[]{:S(2)}) async-start(bf16[8,1024,384]{2,1,0:T(8,128)(2,1)} %bitcast.330), calls=%async_computation.1 | async-start | bytes 12582912 | tf_op jit(solution)/shard_map/all_to_all | solution.py:138
  638.3 53.9 %reduce-scatter.3.cloned.1.call-start = ((), (), s32[]{:S(2)}) async-start(), calls=%async_computation.6 | async-start | bytes 1966080 | tf_op jit(solution)/shard_map/reduce_scatter | solution.py:165
  655.3 37.0 %copy-start.27 = (f32[4,1,2,384,128]{4,3,2,1,0:T(8,128)S(1)}, f32[4,1,2,384,128]{4,3,2,1,0:T(8,128)}, u32[]{:S(2)}) copy-start(f32[4,1,2,384,128]{4,3,2,1,0:T(8,128)} %param.23) | copy-start | bytes 4718596
  655.3 660.0 %all-reduce.7.cloned.1.call-start = ((), (), s32[]{:S(2)}) async-start(), calls=%async_computation.9 | async-start | bytes 4743168
  770.0 21.4 %copy-start.40 = (f32[2048,2]{0,1:T(2,128)S(1)}, f32[2048,2]{0,1:T(2,128)}, u32[]{:S(2)}) copy-start(f32[2048,2]{0,1:T(2,128)} %copy-done.39) | copy-start | bytes 49156
  770.0 21.4 %copy-start.50 = (f32[2048]{0:T(1024)S(1)}, f32[2048]{0:T(1024)}, u32[]{:S(2)}) copy-start(f32[2048]{0:T(1024)} %copy-done.49) | copy-start | bytes 24580
  770.0 21.4 %copy-start.61 = (f32[2048]{0:T(1024)S(1)}, f32[2048]{0:T(1024)}, u32[]{:S(2)}) copy-start(f32[2048]{0:T(1024)} %copy-done.60) | copy-start | bytes 24580
  770.0 21.5 %copy-start.48 = (s32[2048,2]{0,1:T(2,128)S(1)}, s32[2048,2]{0,1:T(2,128)}, u32[]{:S(2)}) copy-start(s32[2048,2]{0,1:T(2,128)} %param.17) | copy-start | bytes 49156
  770.0 24.2 %copy-start.3 = (f32[2048,384]{0,1:T(8,128)S(1)}, f32[2048,384]{0,1:T(8,128)}, u32[]{:S(2)}) copy-start(f32[2048,384]{0,1:T(8,128)} %copy-done.2) | copy-start | bytes 9437188
  770.0 24.1 %copy-start.63 = (f32[2048]{0:T(1024)S(1)}, f32[2048]{0:T(1024)}, u32[]{:S(2)}) copy-start(f32[2048]{0:T(1024)} %copy-done.62) | copy-start | bytes 24580
  770.0 24.1 %copy-start.71 = (f32[384]{0:T(512)S(1)}, f32[384]{0:T(512)}, u32[]{:S(2)}) copy-start(f32[384]{0:T(512)} %get-tuple-element.304) | copy-start | bytes 4612
  789.8 4.4 copy-start.36
  799.3 3.6 copy-start.73
  802.8 6.0 copy-start.9
  850.8 23.3 %copy-start.29 = (bf16[2,1024,6,64]{1,3,2,0:T(8,128)(2,1)S(1)}, bf16[2,1024,6,64]{1,3,2,0:T(8,128)(2,1)}, u32[]{:S(2)}) copy-start(bf16[2,1024,6,64]{1,3,2,0:T(8,128)(2,1)} %get-tuple-element.631) | copy-start | bytes 4718596 | tf_op jit(solution)/shard_map/while
  887.6 8.9 copy-start
  905.5 27.8 %copy-start.1 = (f32[1,1024,6,64]{1,0,3,2:T(1,128)S(1)}, f32[1,1024,6,64]{1,0,3,2:T(1,128)}, u32[]{:S(2)}) copy-start(f32[1,1024,6,64]{1,0,3,2:T(1,128)} %copy.204) | copy-start | bytes 4718596 | tf_op jit(solution)/shard_map/while
  995.9 23.3 %copy-start.29 = (bf16[2,1024,6,64]{1,3,2,0:T(8,128)(2,1)S(1)}, bf16[2,1024,6,64]{1,3,2,0:T(8,128)(2,1)}, u32[]{:S(2)}) copy-start(bf16[2,1024,6,64]{1,3,2,0:T(8,128)(2,1)} %get-tuple-element.631) | copy-start | bytes 4718596 | tf_op jit(solution)/shard_map/while
  1032.7 8.9 copy-start
  1050.6 27.8 %copy-start.1 = (f32[1,1024,6,64]{1,0,3,2:T(1,128)S(1)}, f32[1,1024,6,64]{1,0,3,2:T(1,128)}, u32[]{:S(2)}) copy-start(f32[1,1024,6,64]{1,0,3,2:T(1,128)} %copy.204) | copy-start | bytes 4718596 | tf_op jit(solution)/shard_map/while
  1115.0 5.7 copy-start.26
  1129.0 4.1 copy-start.55
  1129.0 4.2 copy-start.16
  1133.1 3.7 copy-start.80
  1184.6 130.7 %copy-start.38 = (f32[18528]{0:T(1024)S(1)}, f32[18528]{0:T(1024)}, u32[]{:S(2)}) copy-start(f32[18528]{0:T(1024)} %copy-done.37) | copy-start | bytes 222340
  1184.6 130.7 %copy-start.44 = (f32[18528]{0:T(1024)S(1)}, f32[18528]{0:T(1024)}, u32[]{:S(2)}) copy-start(f32[18528]{0:T(1024)} %get-tuple-element.296) | copy-start | bytes 222340
  1184.6 130.7 %copy-start.45 = (f32[18528]{0:T(1024)S(1)}, f32[18528]{0:T(1024)}, u32[]{:S(2)}) copy-start(f32[18528]{0:T(1024)} %get-tuple-element.297) | copy-start | bytes 222340
  1184.6 132.4 %copy-start.43 = (f32[18528]{0:T(1024)S(1)}, f32[18528]{0:T(1024)}, u32[]{:S(2)}) copy-start(f32[18528]{0:T(1024)} %get-tuple-element.299) | copy-start | bytes 222340
  (35 other events, 70.1 us)
Sparse Core Ops, SparseCore 0:
  14.0 132.7 all-reduce.4
  572.4 24.7 reduce-scatter.4
  655.4 36.7 reduce-scatter.2
  1180.7 134.5 all-reduce.6
where the time goes:
time: 1340 us; the launch traced here: 1330 us
  local copies, waits for them, and re-layouts  366 us (27%)
  waiting for transfers between devices  299 us (22%)
  matrix products  294 us (22%)
  other arithmetic  186 us (14%)
  blocking collectives  147 us (11%)
  between operations  16.3 us (1%)
  starting transfers between devices  14.7 us (1%)
    unnamed x6, waiting for transfers between devices  199 us
    dynamic_update_slice x8, local copies, waits for them, and re-layouts, local(): lax.map(partial(attend_backward, score_bias), (seq_queries, seq_keys, seq...  122 us
    all_to_all x1, blocking collectives, to_experts(): lax.all_to_all(outgoing, 'exp', split_axis=0, concat_axis=0, tiled=True)  74.9 us
    dot_general x4, matrix products, raw_scores(): jnp.einsum('qhd,khd->hqk', queries, key_rows, preferred_element_type=jnp....  67.9 us
    dot_general x6, matrix products, right_product(): lax.dot_general(left, right, (((1,), (1,)), ((), ())), preferred_element_...  54.4 us
    all_to_all x2, waiting for transfers between devices, from_experts(): lax.all_to_all(results, 'exp', split_axis=0, concat_axis=0, tiled=True)  50.4 us
    reduce_sum x2, other arithmetic, attend_backward(): jnp.sum(jnp.where(same_var, score_grads, 0.0), axis=(1, 2))  46.5 us
    psum x1, blocking collectives, local(): lax.psum(jnp.concatenate([grad_gain_one, grad_gain_two, grad_bias.reshape...  39.5 us
  transfers between devices with their start and end apart: 7, of which 5 were waited for; matrix products, arithmetic and copies ran while one was open for 14% of the time, Pallas kernels for 0%

commit v1 on v0

v1 whole, which is shorter than its diff:
```python
from functools import partial
import math

import jax
import jax.numpy as jnp
from jax import lax
from jax.experimental import pallas as pl
from jax.experimental.pallas import tpu as pltpu
from jax.sharding import PartitionSpec as P

D = 384
HEADS = 6
HD = 64
PAIRS = HEADS // 2
TOP = 2
SEQ = 1024
LANES = 128
QB = 128
CH = 256
NBLK = SEQ // QB
WIN = 128
SLOT = 256
XW = 2 * D + LANES
SEG_IDS = 8
VAR_IDS = 4
LSE_LANE = SEG_IDS + 6 * VAR_IDS
FAR = 2.0**100
VMEM_BYTES = 60 * 1024 * 1024

norm_epsilon = 1e-06
moment_rate = 0.5
average_rate = 0.9
adam_epsilon = 1e-08
weight_decay = 0.1
rate_dense = 0.05
rate_expert = 0.04
rate_small = 0.2

bf16 = jnp.bfloat16
f32 = jnp.float32


def mm(left, right):
    return lax.dot_general(left, right, (((1,), (0,)), ((), ())), preferred_element_type=f32)


def mm_nt(left, right):
    return lax.dot_general(left, right, (((1,), (1,)), ((), ())), preferred_element_type=f32)


def mm_tn(left, right):
    return lax.dot_general(left, right, (((0,), (0,)), ((), ())), preferred_element_type=f32)


def lane_ids(shape):
    return lax.broadcasted_iota(jnp.int32, shape, len(shape) - 1)


def row_ids(shape):
    return lax.broadcasted_iota(jnp.int32, shape, 0)


def three_pieces(value):
    high = value.astype(bf16)
    rest = value - high.astype(f32)
    middle = rest.astype(bf16)
    low = (rest - middle.astype(f32)).astype(bf16)
    return high.astype(f32), middle.astype(f32), low.astype(f32)


def swap_halves(values):
    lane = lane_ids(values.shape)
    return jnp.where(
        lane % HD < HD // 2,
        pltpu.roll(values, LANES - HD // 2, 1),
        pltpu.roll(values, HD // 2, 1),
    )


def call(kernel, **kwargs):
    return pl.pallas_call(
        kernel,
        compiler_params=pltpu.CompilerParams(
            vmem_limit_bytes=VMEM_BYTES, dimension_semantics=("arbitrary",)
        ),
        **kwargs,
    )


def whole(shape):
    return pl.BlockSpec(shape, lambda *_: (0,) * len(shape))


def cost(flops, moved):
    return pl.CostEstimate(flops=int(flops), transcendentals=0, bytes_accessed=int(moved))


def unpack_kernel(place, shards, in_out, out_out, router_out, flat, spread, *, shard, experts, n_tp):
    rows = shards.shape[1]
    n_dev = shards.shape[0]
    flat[...] = jnp.zeros(flat.shape, f32)
    lane = lane_ids((rows, LANES))
    for s in range(n_dev):
        rel = (lax.bitwise_xor(s // n_tp, place[0])) * n_tp + lax.bitwise_xor(s % n_tp, place[1])
        start, off = divmod(shard * s, LANES)
        piece = shards[rel].astype(f32)
        if off:
            piece = pltpu.roll(piece, off, 1)
            flat[start : start + rows] += jnp.where(lane >= off, piece, 0.0)
            flat[start + 1 : start + 1 + rows] += jnp.where(lane < off, piece, 0.0)
        else:
            flat[start : start + rows] += piece
    for j in range(9):
        in_out[:, j * LANES : (j + 1) * LANES] = flat[pl.ds(j, D, stride=9), :].astype(bf16)
    for j in range(3):
        out_out[:, j * LANES : (j + 1) * LANES] = flat[pl.ds(9 * D + j, D, stride=3), :].astype(bf16)
    share = LANES // experts
    count = D // share
    for i in range(share):
        spread[pl.ds(i, count, stride=share), :] = flat[12 * D : 12 * D + count, :]
    lanes = lane_ids((D, LANES))
    kept = jnp.where(lanes // experts == row_ids((D, LANES)) % share, spread[...], 0.0).astype(bf16)
    fold_lane = lane_ids((LANES, LANES))
    fold = (row_ids((LANES, LANES)) % experts == lax.bitwise_xor(fold_lane, place[0])) & (
        fold_lane < experts
    )
    router_out[...] = mm(kept, jnp.where(fold, 1.0, 0.0).astype(bf16)).astype(bf16)


def unpack_dense(place, shards, shard, experts, n_tp):
    total = shard * shards.shape[0] // LANES
    flat_rows = total + shards.shape[1] + 8
    return call(
        partial(unpack_kernel, shard=shard, experts=experts, n_tp=n_tp),
        grid_spec=pltpu.PrefetchScalarGridSpec(
            num_scalar_prefetch=1,
            grid=(1,),
            in_specs=[whole(shards.shape)],
            out_specs=[whole((D, 3 * D)), whole((D, D)), whole((D, LANES))],
            scratch_shapes=[pltpu.VMEM((flat_rows, LANES), f32), pltpu.VMEM((D, LANES), f32)],
        ),
        out_shape=[
            jax.ShapeDtypeStruct((D, 3 * D), bf16),
            jax.ShapeDtypeStruct((D, D), bf16),
            jax.ShapeDtypeStruct((D, LANES), bf16),
        ],
        cost_estimate=cost(1e8, 4e6),
        name="unpack_dense",
    )(place, shards)


def key_features(marks):
    lane = lane_ids(marks.shape)
    flip = (lane < SEG_IDS) | ((lane >= SEG_IDS + 3 * VAR_IDS) & (lane < LSE_LANE))
    return jnp.where(flip, 1.0 - marks, marks)


def window(win, row, block):
    at = (row * NBLK + block) * 2
    return win[at], win[at + 1]


def in_windows(start, count, step):
    @pl.when(count <= 3)
    def _():
        step(pl.multiple_of(jnp.minimum(start, NBLK - 3) * QB, QB), 3 * QB)

    @pl.when((count > 3) & (count <= 5))
    def _():
        step(pl.multiple_of(jnp.minimum(start, NBLK - 5) * QB, QB), 5 * QB)

    @pl.when(count > 5)
    def _():
        step(0, SEQ)


def forward_kernel(
    win, tokens, cot, cos_ref, sin_ref, marks_ref, routes_ref, gain_one, gain_two, biases,
    in_proj, out_proj, router,
    q_out, k_out, v_out, feat_out, mixed_out, middle_out, rows_out, probs_out,
    keys_aug, values_aug, *, experts,
):
    row = pl.program_id(0)
    for p in range(PAIRS):
        values_aug[p, :, LANES:] = jnp.ones((SEQ, LANES), bf16)

    def project(c, carry):
        at = pl.ds(pl.multiple_of(c * CH, CH), CH)
        x = tokens[at, :].astype(f32)
        factor = lax.rsqrt(jnp.mean(x * x, axis=-1, keepdims=True) + norm_epsilon)
        normed = (x * factor * gain_one[...]).astype(bf16)
        projected = mm(normed, in_proj[...])
        cosine, sine = cos_ref[at, :], sin_ref[at, :]
        features = key_features(marks_ref[at, :].astype(f32)).astype(bf16)
        for j in range(2 * PAIRS):
            part = projected[:, j * LANES : (j + 1) * LANES]
            turned = part * cosine + swap_halves(part) * sine
            if j < PAIRS:
                q_out[at, j * LANES : (j + 1) * LANES] = (
                    turned.astype(bf16) * jnp.asarray(HD**-0.5, bf16)
                )
            else:
                p = j - PAIRS
                turned = turned.astype(bf16)
                k_out[at, p * LANES : (p + 1) * LANES] = turned
                keys_aug[p, at, :LANES] = turned
                keys_aug[p, at, LANES:] = features
        for p in range(PAIRS):
            part = projected[:, 2 * D + p * LANES : 2 * D + (p + 1) * LANES].astype(bf16)
            v_out[at, p * LANES : (p + 1) * LANES] = part
            values_aug[p, at, :LANES] = part
        return carry

    lax.fori_loop(0, SEQ // CH, project, 0)

    lane = lane_ids((QB, LANES))
    first = jnp.where(lane_ids((1, LANES)) < HD, 1.0, 0.0).astype(bf16)
    second = jnp.where(lane_ids((1, LANES)) >= HD, 1.0, 0.0).astype(bf16)

    def attend(block, carry):
        at = pl.ds(pl.multiple_of(block * QB, QB), QB)
        start, count = window(win, row, block)
        marks = marks_ref[at, :].astype(f32)

        def step(key_start, keys):
            key_at = pl.ds(key_start, keys)
            for p in range(PAIRS):
                queries = q_out[at, p * LANES : (p + 1) * LANES]
                feat = [marks * biases[2 * p + i : 2 * p + i + 1, :] for i in range(2)]
                stacked = jnp.concatenate(
                    [
                        jnp.concatenate([queries * first, feat[0].astype(bf16)], axis=1),
                        jnp.concatenate([queries * second, feat[1].astype(bf16)], axis=1),
                    ],
                    axis=0,
                )
                scores = mm_nt(stacked, keys_aug[p, key_at, :])
                top = jnp.max(scores, axis=1, keepdims=True)
                weights = jnp.exp(scores - top).astype(bf16)
                sums = mm(weights, values_aug[p, key_at, :])
                total = sums[:, LANES:]
                mixed = sums[:, :LANES] / total
                mixed_out[at, p * LANES : (p + 1) * LANES] = jnp.where(
                    lane < HD, mixed[:QB], mixed[QB:]
                ).astype(bf16)
                summary = -(top + jnp.log(total))
                high, middle, low = three_pieces(summary)
                for i in range(2):
                    part = slice(i * QB, (i + 1) * QB)
                    feat_out[2 * p + i, at, :] = jnp.where(
                        lane == LSE_LANE,
                        high[part],
                        jnp.where(
                            lane == LSE_LANE + 1,
                            middle[part],
                            jnp.where(lane == LSE_LANE + 2, low[part], feat[i]),
                        ),
                    ).astype(bf16)

        in_windows(start, count, step)
        return carry

    lax.fori_loop(0, NBLK, attend, 0)

    def finish(c, carry):
        at = pl.ds(pl.multiple_of(c * CH, CH), CH)
        middle = tokens[at, :].astype(f32) + mm(mixed_out[at, :], out_proj[...])
        middle_out[at, :] = middle
        factor = lax.rsqrt(jnp.mean(middle * middle, axis=-1, keepdims=True) + norm_epsilon)
        normed = (middle * factor * gain_two[...]).astype(bf16)
        rows_out[at, :D] = normed
        rows_out[at, D : 2 * D] = cot[at, :]
        logits = mm(normed, router[...])
        lanes = lane_ids((CH, LANES))
        named = (lanes == routes_ref[at, 0:1]) | (lanes == routes_ref[at, 1:2])
        top = jnp.max(jnp.where(named, logits, -3.0e38), axis=1, keepdims=True)
        weights = jnp.where(named, jnp.exp(jnp.where(named, logits - top, 0.0)), 0.0)
        probs = weights / jnp.sum(weights, axis=1, keepdims=True)
        probs_out[at, :] = probs
        high, mid, low = three_pieces(probs)
        rows_out[at, 2 * D :] = (
            high + pltpu.roll(mid, experts, 1) + pltpu.roll(low, 2 * experts, 1)
        ).astype(bf16)
        return carry

    lax.fori_loop(0, SEQ // CH, finish, 0)


def forward(win, tokens, cot, cosine, sine, marks, routes, gain_one, gain_two, biases, weights, experts):
    tok = tokens.shape[0]
    seqs = tok // SEQ

    def rows(width):
        return pl.BlockSpec((SEQ, width), lambda i, *_: (i, 0))

    in_proj, out_proj, router = weights
    return call(
        partial(forward_kernel, experts=experts),
        grid_spec=pltpu.PrefetchScalarGridSpec(
            num_scalar_prefetch=1,
            grid=(seqs,),
            in_specs=[
                rows(D), rows(D), rows(LANES), rows(LANES), rows(LANES), rows(TOP),
                whole((1, D)), whole((1, D)), whole((8, LANES)),
                whole((D, 3 * D)), whole((D, D)), whole((D, LANES)),
            ],
            out_specs=[
                rows(D), rows(D), rows(D),
                pl.BlockSpec((HEADS, SEQ, LANES), lambda i, *_: (0, i, 0)),
                rows(D), rows(D), rows(XW), rows(LANES),
            ],
            scratch_shapes=[
                pltpu.VMEM((PAIRS, SEQ, 2 * LANES), bf16),
                pltpu.VMEM((PAIRS, SEQ, 2 * LANES), bf16),
            ],
        ),
        out_shape=[
            jax.ShapeDtypeStruct((tok, D), bf16),
            jax.ShapeDtypeStruct((tok, D), bf16),
            jax.ShapeDtypeStruct((tok, D), bf16),
            jax.ShapeDtypeStruct((HEADS, tok, LANES), bf16),
            jax.ShapeDtypeStruct((tok, D), bf16),
            jax.ShapeDtypeStruct((tok, D), f32),
            jax.ShapeDtypeStruct((tok, XW), bf16),
            jax.ShapeDtypeStruct((tok, LANES), f32),
        ],
        cost_estimate=cost(2e10, 2e7),
        name="attention_forward",
    )(win, tokens, cot, cosine, sine, marks, routes, gain_one, gain_two, biases, *weights)


def experts_kernel(table, *refs, group, experts, blocks):
    weights = refs[: len(group)]
    rows, place_lanes, place_rows = refs[len(group) : len(group) + 3]
    part_out = refs[len(group) + 3]
    grads = refs[len(group) + 4 : 2 * len(group) + 4]
    slots, grad_in, grad_down, total = refs[2 * len(group) + 4 :]
    ff = grad_down.shape[0]

    def first_slot(block, r):
        return pl.multiple_of(table[block * experts + r], 16)

    def windows(block):
        return table[blocks * experts + block]

    tail = blocks - 1
    for g in range(len(group)):
        slots[g, 0:16, :] = jnp.zeros((16, XW), bf16)

    def gather(block, carry):
        at = pl.ds(pl.multiple_of(block * CH, CH), CH)
        source = rows[at, :]

        def picked(w):
            slot = row_ids((WIN, CH)).astype(f32) + (w * WIN).astype(f32)
            return mm(
                jnp.concatenate(
                    [
                        jnp.where(place_lanes[r : r + 1, at] == slot, 1.0, 0.0).astype(bf16)
                        for r in group
                    ],
                    axis=0,
                ),
                source,
            ).astype(bf16)

        moved = picked(jnp.int32(0))
        for g, r in enumerate(group):
            start = first_slot(block, r)
            slots[g, pl.ds(start, 16), :] += moved[g * WIN : g * WIN + 16]
            slots[g, pl.ds(start + 16, WIN - 16), :] = moved[g * WIN + 16 : (g + 1) * WIN]

        def more(w, inner):
            moved = picked(w)
            for g, r in enumerate(group):
                slots[g, pl.ds(first_slot(block, r) + w * WIN, WIN), :] = moved[
                    g * WIN : (g + 1) * WIN
                ]
            return inner

        return lax.fori_loop(1, windows(block), more, carry)

    lax.fori_loop(0, blocks, gather, 0)

    for g, r in enumerate(group):
        end = first_slot(tail, r) + windows(tail) * WIN
        slots[g, pl.ds(end, SLOT), :] = jnp.zeros((SLOT, XW), bf16)
        gate_w = jnp.concatenate([weights[g][z, :D, :] for z in range(ff // LANES)], axis=1)
        up_w = jnp.concatenate([weights[g][z, D : 2 * D, :] for z in range(ff // LANES)], axis=1)
        down_w = jnp.concatenate(
            [
                jnp.concatenate(
                    [weights[g][z, (6 + j) * LANES : (7 + j) * LANES, :] for j in range(3)], axis=1
                )
                for z in range(ff // LANES)
            ],
            axis=0,
        )
        grad_in[...] = jnp.zeros(grad_in.shape, f32)
        grad_down[...] = jnp.zeros(grad_down.shape, f32)

        def step(i, carry, g=g, r=r, gate_w=gate_w, up_w=up_w, down_w=down_w):
            at = pl.ds(pl.multiple_of(i * SLOT, SLOT), SLOT)
            x = slots[g, at, :D]
            cot = slots[g, at, D : 2 * D].astype(f32)
            parts = slots[g, at, 2 * D :].astype(f32)
            prob = (
                parts[:, r : r + 1]
                + parts[:, experts + r : experts + r + 1]
                + parts[:, 2 * experts + r : 2 * experts + r + 1]
            )
            gate_pre = mm(x, gate_w)
            up_pre = mm(x, up_w)
            sigmoid = 1.0 / (1.0 + jnp.exp(-gate_pre))
            silu = gate_pre * sigmoid
            hidden = (silu * up_pre).astype(bf16)
            result = mm(hidden, down_w).astype(bf16).astype(f32)
            grad_result = (prob * cot).astype(bf16)
            grad_hidden = mm_nt(grad_result, down_w)
            grad_gate = (
                grad_hidden * up_pre * sigmoid * (1.0 + gate_pre * (1.0 - sigmoid))
            ).astype(bf16)
            grad_up = (grad_hidden * silu).astype(bf16)
            grad_rows = mm_nt(grad_gate, gate_w) + mm_nt(grad_up, up_w)
            grad_in[:, :ff] += mm_tn(x, grad_gate)
            grad_in[:, ff:] += mm_tn(x, grad_up)
            grad_down[...] += mm_tn(hidden, grad_result)
            score = jnp.sum(cot * result, axis=1, keepdims=True)
            high, mid, _ = three_pieces(jnp.broadcast_to(score, (SLOT, LANES)))
            lane = lane_ids((SLOT, LANES))
            slots[g, at, :D] = (prob * result).astype(bf16)
            slots[g, at, D : 2 * D] = grad_rows.astype(bf16)
            slots[g, at, 2 * D :] = jnp.where(
                lane == r, high, jnp.where(lane == experts + r, mid, 0.0)
            ).astype(bf16)
            return carry

        lax.fori_loop(0, table[blocks * experts + blocks + r], step, 0)
        for z in range(ff // LANES):
            cols = slice(z * LANES, (z + 1) * LANES)
            grads[g][z, :D, :] = grad_in[:, cols].astype(bf16)
            grads[g][z, D : 2 * D, :] = grad_in[:, ff + z * LANES : ff + (z + 1) * LANES].astype(bf16)
            for j in range(3):
                grads[g][z, (6 + j) * LANES : (7 + j) * LANES, :] = grad_down[
                    cols, j * LANES : (j + 1) * LANES
                ].astype(bf16)

    def scatter(block, carry):
        at = pl.ds(pl.multiple_of(block * CH, CH), CH)
        places = place_rows[at, :]

        def sent(w):
            slot = lane_ids((CH, WIN)).astype(f32) + (w * WIN).astype(f32)
            pick = jnp.concatenate(
                [jnp.where(places[:, r : r + 1] == slot, 1.0, 0.0).astype(bf16) for r in group],
                axis=1,
            )
            source = jnp.concatenate(
                [slots[g, pl.ds(first_slot(block, r) + w * WIN, WIN), :] for g, r in enumerate(group)],
                axis=0,
            )
            return mm(pick, source)

        total[...] = sent(jnp.int32(0))

        def more(w, inner):
            total[...] += sent(w)
            return inner

        lax.fori_loop(1, windows(block), more, 0)
        part_out[at, :] = total[...].astype(bf16)
        return carry

    lax.fori_loop(0, blocks, scatter, 0)


def run_experts(table, weights, rows, place_lanes, place_rows, group, experts, cap):
    tok = rows.shape[0]
    ff = weights[0].shape[0] * LANES
    blocks = tok // CH
    shape = weights[0].shape
    out = call(
        partial(experts_kernel, group=group, experts=experts, blocks=blocks),
        grid_spec=pltpu.PrefetchScalarGridSpec(
            num_scalar_prefetch=1,
            grid=(1,),
            in_specs=[whole(shape)] * len(group)
            + [whole((tok, XW)), whole(place_lanes.shape), whole((tok, LANES))],
            out_specs=[whole((tok, XW))] + [whole(shape)] * len(group),
            scratch_shapes=[
                pltpu.VMEM((len(group), cap + 4 * WIN + SLOT, XW), bf16),
                pltpu.VMEM((D, 2 * ff), f32),
                pltpu.VMEM((ff, D), f32),
                pltpu.VMEM((CH, XW), f32),
            ],
        ),
        out_shape=[jax.ShapeDtypeStruct((tok, XW), bf16)]
        + [jax.ShapeDtypeStruct(shape, bf16)] * len(group),
        cost_estimate=cost(4e9 * len(group), 3e6 * len(group) + 8e6),
        name="experts",
    )(table, *weights, rows, place_lanes, place_rows)
    return out[0], out[1:]


def backward_kernel(
    win, place, *refs, experts, n_tp, parts, shard,
):
    part_refs = refs[:parts]
    (
        tokens, rows_ref, probs_ref, middle_ref, mixed_ref, q_ref, k_ref, v_ref, feat_ref, marks_ref,
        cos_ref, sin_ref, gain_one, gain_two, in_proj, out_proj, router,
        block_out, grad_in_out, dense_out, gain_out, bias_out,
        grad_middle, grad_mixed, keys_aug, values_aug, grad_q, grad_k, grad_v,
        grad_in_proj, grad_out_proj, grad_router, flat,
    ) = refs[parts:]
    row = pl.program_id(0)

    @pl.when(row == 0)
    def _():
        grad_in_proj[...] = jnp.zeros(grad_in_proj.shape, f32)
        grad_out_proj[...] = jnp.zeros(grad_out_proj.shape, f32)
        grad_router[...] = jnp.zeros(grad_router.shape, f32)
        gain_out[...] = jnp.zeros(gain_out.shape, f32)
        bias_out[...] = jnp.zeros(bias_out.shape, f32)

    fold_row, fold_lane = row_ids((LANES, LANES)), lane_ids((LANES, LANES))
    tile = jnp.where(
        (lax.bitwise_xor(fold_row, place[0]) == fold_lane % experts) & (fold_row < experts), 1.0, 0.0
    ).astype(bf16)

    def head(c, carry):
        at = pl.ds(pl.multiple_of(c * CH, CH), CH)
        back = part_refs[0][at, :].astype(f32)
        for ref in part_refs[1:]:
            back = back + ref[at, :].astype(f32)
        middle = middle_ref[at, :]
        block_out[at, :] = (middle + back[:, :D]).astype(bf16)
        scores = back[:, 2 * D :]
        scores = scores + pltpu.roll(scores, LANES - experts, 1)
        probs = probs_ref[at, :]
        inner = jnp.sum(probs * scores, axis=1, keepdims=True)
        grad_logits = (probs * (scores - inner)).astype(bf16)
        grad_normed = mm_nt(grad_logits, router[...]) + back[:, D : 2 * D]
        grad_router[...] += mm_tn(rows_ref[at, :D], mm(grad_logits, tile).astype(bf16))
        factor = lax.rsqrt(jnp.mean(middle * middle, axis=-1, keepdims=True) + norm_epsilon)
        weighted = grad_normed * gain_two[...]
        gain_out[1:2, :] += jnp.sum(grad_normed * middle * factor, axis=0, keepdims=True)
        cot = rows_ref[at, D : 2 * D].astype(f32)
        grad = (
            cot
            + factor * weighted
            - middle
            * (factor * factor * factor)
            * jnp.mean(weighted * middle, axis=-1, keepdims=True)
        )
        grad_middle[at, :] = grad
        branch = grad.astype(bf16)
        grad_out_proj[...] += mm_tn(mixed_ref[at, :], branch)
        grad_mixed[at, :] = mm_nt(branch, out_proj[...]).astype(bf16)
        features = key_features(marks_ref[at, :].astype(f32)).astype(bf16)
        for p in range(PAIRS):
            cols = slice(p * LANES, (p + 1) * LANES)
            keys_aug[p, at, :LANES] = k_ref[at, cols]
            keys_aug[p, at, LANES:] = features
            values_aug[p, at, :LANES] = v_ref[at, cols]
            values_aug[p, at, LANES:] = features
        return carry

    lax.fori_loop(0, SEQ // CH, head, 0)
    grad_k[...] = jnp.zeros(grad_k.shape, f32)
    grad_v[...] = jnp.zeros(grad_v.shape, f32)

    lane = lane_ids((QB, LANES))
    first = jnp.where(lane_ids((1, LANES)) < HD, 1.0, 0.0).astype(bf16)
    second = jnp.where(lane_ids((1, LANES)) >= HD, 1.0, 0.0).astype(bf16)

    def attend(block, carry):
        at = pl.ds(pl.multiple_of(block * QB, QB), QB)
        start, count = window(win, row, block)
        marks = marks_ref[at, :].astype(f32)

        def step(key_start, keys):
            key_at = pl.ds(key_start, keys)
            for p in range(PAIRS):
                cols = slice(p * LANES, (p + 1) * LANES)
                queries = q_ref[at, cols]
                out_grad = grad_mixed[at, cols]
                product = out_grad.astype(f32) * mixed_ref[at, cols].astype(f32)
                q_rows, g_rows = [], []
                for i, mask in enumerate((first, second)):
                    inside = (lane < HD) if i == 0 else (lane >= HD)
                    inner = -jnp.sum(jnp.where(inside, product, 0.0), axis=1, keepdims=True)
                    high, middle, low = three_pieces(jnp.broadcast_to(inner, (QB, LANES)))
                    extra = jnp.where(
                        lane == LSE_LANE,
                        high,
                        jnp.where(
                            lane == LSE_LANE + 1,
                            middle,
                            jnp.where(lane == LSE_LANE + 2, low, 0.0),
                        ),
                    ).astype(bf16)
                    q_rows.append(
                        jnp.concatenate([queries * mask, feat_ref[2 * p + i, at, :]], axis=1)
                    )
                    g_rows.append(jnp.concatenate([out_grad * mask, extra], axis=1))
                stacked = jnp.concatenate(q_rows, axis=0)
                grads = jnp.concatenate(g_rows, axis=0)
                keys_here = keys_aug[p, key_at, :]
                probs = jnp.exp(mm_nt(keys_here, stacked))
                shifted = mm_nt(values_aug[p, key_at, :], grads)
                grad_scores = (probs * shifted).astype(bf16)
                grad_v[key_at, cols] += mm(probs.astype(bf16), grads[:, :LANES])
                grad_k[key_at, cols] += mm(grad_scores, stacked[:, :LANES])
                back = mm_tn(grad_scores, keys_here)
                grad_q[at, cols] = (
                    jnp.where(lane < HD, back[:QB, :LANES], back[QB:, :LANES]) * HD**-0.5
                )
                for i in range(2):
                    bias_out[2 * p + i : 2 * p + i + 1, :] += jnp.sum(
                        marks * back[i * QB : (i + 1) * QB, LANES:], axis=0, keepdims=True
                    )

        in_windows(start, count, step)
        return carry

    lax.fori_loop(0, NBLK, attend, 0)

    def tail(c, carry):
        at = pl.ds(pl.multiple_of(c * CH, CH), CH)
        cosine, sine = cos_ref[at, :], sin_ref[at, :]
        pieces = []
        for ref in (grad_q, grad_k):
            for p in range(PAIRS):
                part = ref[at, p * LANES : (p + 1) * LANES]
                pieces.append((part * cosine - swap_halves(part) * sine).astype(bf16))
        pieces.append(grad_v[at, :].astype(bf16))
        grad_projected = jnp.concatenate(pieces, axis=1)
        x = tokens[at, :].astype(f32)
        factor = lax.rsqrt(jnp.mean(x * x, axis=-1, keepdims=True) + norm_epsilon)
        normed = (x * factor * gain_one[...]).astype(bf16)
        grad_in_proj[...] += mm_tn(normed, grad_projected)
        grad_normed = mm_nt(grad_projected, in_proj[...])
        weighted = grad_normed * gain_one[...]
        gain_out[0:1, :] += jnp.sum(grad_normed * x * factor, axis=0, keepdims=True)
        grad_in_out[at, :] = (
            grad_middle[at, :]
            + factor * weighted
            - x * (factor * factor * factor) * jnp.mean(weighted * x, axis=-1, keepdims=True)
        ).astype(bf16)
        return carry

    lax.fori_loop(0, SEQ // CH, tail, 0)

    @pl.when(row == pl.num_programs(0) - 1)
    def _():
        for j in range(9):
            flat[pl.ds(j, D, stride=9), :] = grad_in_proj[:, j * LANES : (j + 1) * LANES]
        for j in range(3):
            flat[pl.ds(9 * D + j, D, stride=3), :] = grad_out_proj[:, j * LANES : (j + 1) * LANES]
        share = LANES // experts
        count = D // share
        lanes = lane_ids((D, LANES))
        grad_router[...] = jnp.where(
            lanes // experts == row_ids((D, LANES)) % share, grad_router[...], 0.0
        )
        merged = grad_router[pl.ds(0, count, stride=share), :]
        for i in range(1, share):
            merged = merged + grad_router[pl.ds(i, count, stride=share), :]
        flat[12 * D : 12 * D + count, :] = merged
        spare = flat.shape[0] - (12 * D + count)
        flat[12 * D + count :, :] = jnp.zeros((spare, LANES), f32)
        n_dev = dense_out.shape[0]
        rows = dense_out.shape[1]
        half = n_dev // 2
        piece_lane = lane_ids((rows, LANES))
        for s in range(n_dev):
            exp_rel = lax.bitwise_xor(s // n_tp, place[0])
            rel = (
                (exp_rel % 2) * half + (exp_rel // 2) * n_tp + lax.bitwise_xor(s % n_tp, place[1])
            )
            start, off = divmod(shard * s, LANES)
            piece = flat[start : start + rows, :]
            if off:
                piece = jnp.where(
                    piece_lane < LANES - off,
                    pltpu.roll(piece, LANES - off, 1),
                    pltpu.roll(flat[start + 1 : start + 1 + rows, :], LANES - off, 1),
                )
            dense_out[rel] = piece.astype(bf16)


def backward(win, place, parts, tokens, saved, marks, cosine, sine, gains, weights, sizes):
    experts, n_exp, n_tp, shard, shard_rows = sizes
    q, k, v, feat, mixed, middle, rows_arr, probs = saved
    tok = tokens.shape[0]

    def rows(width):
        return pl.BlockSpec((SEQ, width), lambda i, *_: (i, 0))

    flat_rows = shard * n_exp * n_tp // LANES + shard_rows + 8
    return call(
        partial(backward_kernel, experts=experts, n_tp=n_tp, parts=len(parts), shard=shard),
        grid_spec=pltpu.PrefetchScalarGridSpec(
            num_scalar_prefetch=2,
            grid=(tok // SEQ,),
            in_specs=[rows(XW)] * len(parts)
            + [
                rows(D), rows(XW), rows(LANES), rows(D), rows(D), rows(D), rows(D), rows(D),
                pl.BlockSpec((HEADS, SEQ, LANES), lambda i, *_: (0, i, 0)),
                rows(LANES), rows(LANES), rows(LANES), whole((1, D)), whole((1, D)),
                whole((D, 3 * D)), whole((D, D)), whole((D, LANES)),
            ],
            out_specs=[
                rows(D), rows(D), whole((n_exp * n_tp, shard_rows, LANES)), whole((8, D)), whole((8, LANES)),
            ],
            scratch_shapes=[
                pltpu.VMEM((SEQ, D), f32),
                pltpu.VMEM((SEQ, D), bf16),
                pltpu.VMEM((PAIRS, SEQ, 2 * LANES), bf16),
                pltpu.VMEM((PAIRS, SEQ, 2 * LANES), bf16),
                pltpu.VMEM((SEQ, D), f32),
                pltpu.VMEM((SEQ, D), f32),
                pltpu.VMEM((SEQ, D), f32),
                pltpu.VMEM((D, 3 * D), f32),
                pltpu.VMEM((D, D), f32),
                pltpu.VMEM((D, LANES), f32),
                pltpu.VMEM((flat_rows, LANES), f32),
            ],
        ),
        out_shape=[
            jax.ShapeDtypeStruct((tok, D), bf16),
            jax.ShapeDtypeStruct((tok, D), bf16),
            jax.ShapeDtypeStruct((n_exp * n_tp, shard_rows, LANES), bf16),
            jax.ShapeDtypeStruct((8, D), f32),
            jax.ShapeDtypeStruct((8, LANES), f32),
        ],
        cost_estimate=cost(4e10, 3e7),
        name="attention_backward",
    )(
        win, place, *parts, tokens, rows_arr, probs, middle, mixed, q, k, v, feat, marks,
        cosine, sine, *gains, *weights,
    )


def swap(values, axis, mask):
    size = lax.axis_size(axis)
    return lax.ppermute(values, axis, [(i, i ^ mask) for i in range(size)])


def add_up(parts):
    total = parts[0].astype(f32)
    for part in parts[1:]:
        total = total + part.astype(f32)
    return total


def even_sum(parts):
    while len(parts) > 1:
        parts = [parts[i] + parts[i + 1] for i in range(0, len(parts), 2)]
    return parts[0]


def adamw_update(old_state, grad_value, rate, decay, step_value):
    moment_one = moment_rate * old_state[1] + (1.0 - moment_rate) * grad_value
    moment_two = moment_rate * old_state[2] + (1.0 - moment_rate) * grad_value * grad_value
    correction = 1.0 - jnp.power(moment_rate, step_value)
    master = old_state[0] - rate * (
        moment_one / correction / (jnp.sqrt(moment_two / correction) + adam_epsilon)
        + decay * old_state[0]
    )
    average = average_rate * old_state[3] + (1.0 - average_rate) * master
    return jnp.stack([master, moment_one, moment_two, average])


def local(
    tokens, cotangent, routes, segments, variates, positions, step_count,
    dense_state, gate_up_state, down_state, small_state,
):
    tok = tokens.shape[0]
    n_exp, n_tp = lax.axis_size("exp"), lax.axis_size("tp")
    experts = n_exp * gate_up_state.shape[1]
    cap = 2 * tok * TOP // experts
    my_exp, my_tp = lax.axis_index("exp"), lax.axis_index("tp")
    place = jnp.stack([my_exp, my_tp]).astype(jnp.int32)
    shard = dense_state.shape[1]
    shard_rows = -(-shard // (16 * LANES)) * 16

    own = jnp.pad(dense_state[0].astype(bf16), (0, shard_rows * LANES - shard))
    own = own.reshape(1, shard_rows, LANES)
    line = jnp.concatenate([own] + [swap(own, "tp", j) for j in range(1, n_tp)], axis=0)
    plane = [line] + [swap(line, "exp", m) for m in range(2, n_exp, 2)]
    pairs = jnp.stack(plane)
    both = jnp.stack([pairs, swap(pairs, "exp", 1)], axis=1)
    weights = unpack_dense(
        place, both.reshape(n_exp * n_tp, shard_rows, LANES), shard, experts, n_tp
    )

    gate_up = gate_up_state[0, 0].astype(bf16)
    down = down_state[0, 0].astype(bf16)
    gate_up = jnp.concatenate(
        [gate_up] + [swap(gate_up, "tp", j) for j in range(1, n_tp)], axis=2
    )
    down = jnp.concatenate([down] + [swap(down, "tp", j) for j in range(1, n_tp)], axis=0)
    ff = gate_up.shape[2]
    cuts = ff // LANES
    packed = jnp.concatenate(
        [
            gate_up.reshape(2 * D, cuts, LANES).transpose(1, 0, 2),
            down.reshape(cuts, LANES, 3, LANES).transpose(0, 2, 1, 3).reshape(cuts, D, LANES),
        ],
        axis=1,
    )
    expert_weights = {0: packed}
    for m in range(2, n_exp, 2):
        expert_weights[m] = swap(packed, "exp", m)
    for m in range(0, n_exp, 2):
        expert_weights[m + 1] = swap(expert_weights[m], "exp", 1)

    near = lax.bitwise_xor(routes, my_exp.astype(jnp.int32))
    blocks = tok // CH
    ids = jnp.arange(experts, dtype=jnp.int32)
    named = (near[:, 0:1] == ids) | (near[:, 1:2] == ids)
    named_blocks = named.reshape(blocks, CH, experts)
    steps = jnp.arange(CH, dtype=jnp.int32)
    before = (steps[:, None] > steps[None, :]).astype(bf16)
    rank = jnp.einsum(
        "st,bte->bse", before, named_blocks.astype(bf16), preferred_element_type=f32
    )
    counts = jnp.sum(named_blocks.astype(jnp.int32), axis=1)
    block_ids = jnp.arange(blocks, dtype=jnp.int32)
    base = jnp.sum(
        jnp.where((block_ids[:, None] > block_ids[None, :])[:, :, None], counts[None], 0), axis=1
    )
    odd = base % 16
    spot = jnp.where(named_blocks, rank + odd[:, None, :].astype(f32), -1.0).reshape(tok, experts)
    place_lanes = spot.T
    place_rows = jnp.pad(spot, ((0, 0), (0, LANES - experts)), constant_values=-1.0)
    window_counts = jnp.max((odd + counts) // WIN + 1, axis=1)
    slot_steps = (jnp.sum(counts, axis=0) + SLOT - 1) // SLOT
    table = jnp.concatenate([(base - odd).reshape(-1), window_counts, slot_steps])

    seg, var = segments.reshape(tok, 1), variates.reshape(tok, 1)
    lanes = jnp.arange(LANES, dtype=jnp.int32)[None, :]
    marks = jnp.where(
        lanes < SEG_IDS,
        seg == lanes,
        jnp.where(lanes < LSE_LANE, var == lanes % VAR_IDS, lanes < LSE_LANE + 3),
    ).astype(bf16)
    small_params = small_state[0]
    gains = (small_params[:D].reshape(1, D), small_params[D : 2 * D].reshape(1, D))
    score_bias = small_params[2 * D :].reshape(2, HEADS)
    high = lax.reduce_precision(score_bias, 8, 7)
    mid = lax.reduce_precision(score_bias - high, 8, 7)
    low = lax.reduce_precision(score_bias - high - mid, 8, 7)
    pieces = jnp.stack([high, mid, low], axis=1).transpose(2, 0, 1)
    biases = jnp.concatenate(
        [
            jnp.full((HEADS, SEG_IDS), -FAR, f32),
            jnp.repeat(pieces.reshape(HEADS, 6), VAR_IDS, axis=1),
            jnp.zeros((HEADS, LANES - LSE_LANE), f32),
        ],
        axis=1,
    )
    biases = jnp.pad(biases, ((0, 2), (0, 0)))
    head_ids = segments[:, ::QB]
    tail_ids = segments[:, QB - 1 :: QB]
    lowest = jnp.sum((segments[:, None, :] < head_ids[:, :, None]).astype(jnp.int32), axis=2)
    highest = jnp.sum((segments[:, None, :] <= tail_ids[:, :, None]).astype(jnp.int32), axis=2)
    win_start = lowest // QB
    win_count = (highest + QB - 1) // QB - win_start
    win = jnp.stack([win_start, win_count], axis=2).reshape(-1)
    frequency = jnp.exp(jnp.arange(HD // 2, dtype=f32) * (-2.0 * math.log(10000.0) / HD))
    angles = positions.reshape(tok, 1).astype(f32) * jnp.tile(frequency, 4)[None, :]
    cosine = jnp.cos(angles)
    sine = jnp.sin(angles) * jnp.where(lanes % HD < HD // 2, -1.0, 1.0)

    saved = forward(
        win, tokens, cotangent, cosine, sine, marks, near, *gains, biases, weights, experts
    )
    routed = saved[6]
    groups = [(0, 1), (2, 3, 4, 5), (6, 7)] if n_exp == 8 else [
        tuple(range(i, i + 4)) for i in range(0, n_exp, 4)
    ]
    parts, expert_grads = [], {}
    for group in groups:
        part, grads = run_experts(
            table, [expert_weights[r] for r in group], routed, place_lanes, place_rows, group, experts, cap
        )
        parts.append(part)
        expert_grads.update(zip(group, grads))

    if len(parts) > 3:
        parts = [add_up(parts).astype(bf16)]

    block_out, grad_in, dense_grad, gain_grad, bias_grad = backward(
        win, place, parts, tokens, saved, marks, cosine, sine, gains, weights,
        (experts, n_exp, n_tp, shard, shard_rows),
    )

    halves = []
    for m in range(0, n_exp, 2):
        half = add_up([expert_grads[m], swap(expert_grads[m + 1], "exp", 1)])
        halves.append(half.astype(bf16))
    mine = add_up([halves[0]] + [swap(halves[m // 2], "exp", m) for m in range(2, n_exp, 2)])
    mine = mine.astype(bf16)
    mine_in = mine[:, : 2 * D].transpose(1, 0, 2).reshape(2, D, n_tp, ff // n_tp)
    mine_down = (
        mine[:, 2 * D :].reshape(cuts, 3, LANES, LANES).transpose(0, 2, 1, 3)
        .reshape(n_tp, ff // n_tp, D)
    )
    grad_gate_up = add_up(
        [mine_in[:, :, 0]] + [swap(mine_in[:, :, j], "tp", j) for j in range(1, n_tp)]
    )[None]
    grad_down = add_up(
        [mine_down[0]] + [swap(mine_down[j], "tp", j) for j in range(1, n_tp)]
    )[None]

    dense_grad = dense_grad.reshape(2, n_exp // 2, n_tp, shard_rows, LANES)
    dense_half = add_up([dense_grad[0], swap(dense_grad[1], "exp", 1)]).astype(bf16)
    dense_line = add_up(
        [dense_half[0]] + [swap(dense_half[m // 2], "exp", m) for m in range(2, n_exp, 2)]
    ).astype(bf16)
    dense_mine = add_up(
        [dense_line[0]] + [swap(dense_line[j], "tp", j) for j in range(1, n_tp)]
    )
    dense_mine = dense_mine.reshape(-1)[:shard]

    same = jnp.sum(bias_grad[:HEADS, SEG_IDS : SEG_IDS + VAR_IDS], axis=1)
    other_lane = SEG_IDS + 3 * VAR_IDS
    other = jnp.sum(bias_grad[:HEADS, other_lane : other_lane + VAR_IDS], axis=1)
    small_grad = jnp.concatenate([gain_grad[0], gain_grad[1], same, other])
    small_grad = jnp.pad(small_grad, (0, 1024 - small_grad.shape[0])).reshape(8, LANES)
    small_grad = small_grad + swap(small_grad, "exp", 1)
    small_grad = even_sum([small_grad] + [swap(small_grad, "exp", m) for m in range(2, n_exp, 2)])
    small_grad = even_sum([small_grad] + [swap(small_grad, "tp", j) for j in range(1, n_tp)])
    small_grad = small_grad.reshape(-1)[: small_state.shape[1]]

    step_value = step_count[0].astype(f32)
    dense_new = adamw_update(dense_state, dense_mine, rate_dense, weight_decay, step_value)
    gate_up_new = adamw_update(gate_up_state, grad_gate_up, rate_expert, weight_decay, step_value)
    down_new = adamw_update(down_state, grad_down, rate_expert, weight_decay, step_value)
    small_new = adamw_update(small_state, small_grad, rate_small, 0.0, step_value)
    return (
        block_out,
        grad_in,
        dense_new,
        dense_new[0].astype(bf16),
        gate_up_new,
        gate_up_new[0].astype(bf16),
        down_new,
        down_new[0].astype(bf16),
        small_new,
    )


def solution(mesh):
    in_specs = (
        P(("exp", "tp"), None),
        P(("exp", "tp"), None),
        P(("exp", "tp"), None),
        P(("exp", "tp"), None),
        P(("exp", "tp"), None),
        P(("exp", "tp"), None),
        P(),
        P(None, ("exp", "tp")),
        P(None, "exp", None, None, "tp"),
        P(None, "exp", "tp", None),
        P(),
    )
    out_specs = (
        P(("exp", "tp"), None),
        P(("exp", "tp"), None),
        P(None, ("exp", "tp")),
        P(("exp", "tp")),
        P(None, "exp", None, None, "tp"),
        P("exp", None, None, "tp"),
        P(None, "exp", "tp", None),
        P("exp", "tp", None),
        P(),
    )
    return jax.shard_map(local, mesh=mesh, in_specs=in_specs, out_specs=out_specs, check_vma=False)
```

time: 1340 us -> 387 us (0.29)
  local copies, waits for them, and re-layouts: 366 us -> 17.2 us
  matrix products: 294 us -> 0.18 us
  waiting for transfers between devices: 299 us -> 90 us
  Pallas kernels: 0 us -> 181 us
  other arithmetic: 186 us -> 32.1 us
  blocking collectives: 147 us -> 0 us
  starting transfers between devices: 14.7 us -> 60.3 us
  between operations: 16.3 us -> 2.26 us
    dot_general x32 -> x1, matrix products: 294 us -> 0.18 us  [local(): jnp.einsum('st,bte->bse', before, named_blocks.astype(bf16), preferred_el...]
    unnamed x6 -> x0, waiting for transfers between devices: 199 us -> none
    pallas_call x0 -> x6, Pallas kernels: none -> 181 us  [the longest x3 88.5 us: run_experts(): call(partial(experts_kernel, group=group, experts=experts, blocks=blocks)...]
    dynamic_update_slice x8 -> x0, local copies, waits for them, and re-layouts: 122 us -> none  [local(): lax.map(partial(attend_backward, score_bias), (seq_queries, seq_keys, seq...]
    reduce_sum x13 -> x4, other arithmetic: 119 us -> 1.55 us  [the longest x1 0.98 us: local(): same = jnp.sum(bias_grad[:HEADS, SEG_IDS:SEG_IDS + VAR_IDS], axis=1)]
    gather x4 -> x0, local copies, waits for them, and re-layouts: 103 us -> none  [the longest x1 34.8 us: local(): grad_outgoing = jnp.where(filled[:, None], grad_pairs[source], 0)]
    ppermute x0 -> x47, waiting for transfers between devices: none -> 90 us  [swap(): return lax.ppermute(values, axis, [(i, i ^ mask) for i in range(size)])]
    all_to_all x1 -> x0, blocking collectives: 74.9 us -> none  [to_experts(): lax.all_to_all(outgoing, 'exp', split_axis=0, concat_axis=0, tiled=True)]
  transfers between devices with their start and end apart: 7 -> 47, of which waited for: 5 -> 18; matrix products, arithmetic and copies ran while one was open for 14% -> 10% of each run, Pallas kernels for 0% -> 22%
where the time goes in v1:
time: 387 us; the launch traced here: 383 us
  Pallas kernels  181 us (47%)
  waiting for transfers between devices  90 us (23%)
  starting transfers between devices  60.3 us (16%)
  other arithmetic  32.1 us (8%)
  local copies, waits for them, and re-layouts  17.2 us (4%)
    ppermute x47, waiting for transfers between devices, swap(): return lax.ppermute(values, axis, [(i, i ^ mask) for i in range(size)])  90 us
    pallas_call x3, Pallas kernels, run_experts(): call(partial(experts_kernel, group=group, experts=experts, blocks=blocks)...  88.5 us
    ppermute x47, starting transfers between devices, swap(): return lax.ppermute(values, axis, [(i, i ^ mask) for i in range(size)])  60.3 us
    pallas_call x1, Pallas kernels, backward(): call(partial(backward_kernel, experts=experts, n_tp=n_tp, parts=len(parts...  53.7 us
    pallas_call x1, Pallas kernels, forward(): call(partial(forward_kernel, experts=experts), grid_spec=pltpu.PrefetchSc...  34.9 us
  transfers between devices with their start and end apart: 47, of which 18 were waited for; matrix products, arithmetic and copies ran while one was open for 10% of the time, Pallas kernels for 22%

profile of v1, /device:TPU:0, one launch (start us, length us, event | category | flops | bytes accessed | tf_op | source)
XLA Modules:
  0.0 383.0 jit_solution(7555588125942952761)
XLA Ops:
  0.7 2.9 multiply_reduce_fusion.1
  3.6 5.1 %collective-permute-start.9 = (bf16[1,160,128]{2,1,0:T(8,128)(2,1)S(1)}, bf16[1,160,128]{2,1,0:T(8,128)(2,1)S(1)}, u32[]{:S(2)}, u32[]{:S(2)}) collective-permute-start(bf16[1,160,128]{2,1,0:T(8,128)(2,1)S(1)} %pad_bitcast_fusion), channel_id=1, source_target_pairs={{0,3},{1,2},{2,1},{3,0},{4,7},{5,6},{6,5},{7,4},{8,11},{9,10},{10,... | collective-permute-start | bytes 122888 | tf_op jit(solution)/shard_map/ppermute | solution.py:748
  9.3 1.0 bitcast_convert_fusion
  10.4 3.8 collective-permute-start.2
  16.2 1.3 fusion.53
  20.4 2.4 fusion.5.marks_ref.refs_12_
  23.3 3.8 collective-permute-start
  27.3 3.9 %collective-permute-start.3 = (bf16[128,384]{0,1:T(8,128)(2,1)S(1)}, bf16[128,384]{0,1:T(8,128)(2,1)S(1)}, u32[]{:S(2)}, u32[]{:S(2)}) collective-permute-start(bf16[128,384]{0,1:T(8,128)(2,1)S(1)} %bitcast_convert_fusion.1), channel_id=1, source_target_pairs={{0,1},{1,0},{2,3},{3,2},{4,5},{5,4},{6,7},{7,6},{8,9},{9,8},{10,11... | collective-permute-start | bytes 294920 | tf_op jit(solution)/shard_map/ppermute | solution.py:748
  31.1 1.5 fusion.42
  32.7 6.2 %collective-permute-done.4 = bf16[128,384]{0,1:T(8,128)(2,1)S(1)} collective-permute-done((bf16[128,384]{0,1:T(8,128)(2,1)S(1)}, bf16[128,384]{0,1:T(8,128)(2,1)S(1)}, u32[]{:S(2)}, u32[]{:S(2)}) %collective-permute-start.4) | collective-permute-done | bytes 98336 | tf_op jit(solution)/shard_map/ppermute | solution.py:748
  38.9 1.5 collective-permute-start.11
  40.4 1.5 collective-permute-start.10
  43.4 2.5 collective-permute-start.18
  45.9 1.9 collective-permute-done.10
  47.9 2.9 collective-permute-done.12
  50.8 2.0 fusion.45
  56.1 1.1 pad.18.refs_4_.refs_6_
  57.7 5.6 %fusion.3 = (f32[2048,128]{1,0:T(8,128)}, f32[2048,128]{1,0:T(8,128)}) fusion(f32[128]{0:T(128)S(1)} %compare_select_fusion.2, f32[128]{0:T(128)S(1)} %mul.218, f32[2048]{0:T(1024)S(1)} %bitcast.230), kind=kLoop, calls=%fused_computation.15 | loop fusion | flops 524288 | bytes 2106368 | tf_op jit(solution)/shard_map/mul | solution.py:876
  63.3 2.1 collective-permute-start.16
  65.4 1.5 collective-permute-start.14
  66.9 2.3 pad_maximum_fusion.1
  69.2 3.8 unpack_dense.1
  73.0 3.1 collective-permute-done.18.refs_0_
  76.1 34.9 %attention_forward.1 = (bf16[2048,384]{1,0:T(8,128)(2,1)}, bf16[2048,384]{1,0:T(8,128)(2,1)}, bf16[2048,384]{1,0:T(8,128)(2,1)}, bf16[6,2048,128]{2,1,0:T(8,128)...) custom-call(s32[32]{0:T(128)} %reshape.447.win, ...), custom_call_target="tpu_custom_call" | custom-call | flops 20000000000 | bytes 20000000 | tf_op jit(solution)/shard_map/attention_forward/pallas_call | solution.py:297
  111.1 1.6 collective-permute-start.17
  112.7 25.2 %experts.3 = (bf16[2048,896]{1,0:T(8,128)(2,1)}, bf16[4,1152,128]{2,1,0:T(8,128)(2,1)}, bf16[4,1152,128]{2,1,0:T(8,128)(2,1)}) custom-call(s32[80]{0:T(128)} %pad_add_fusion.2.table, bf16[4,1152,128]{2,1,0:T(8,128)(2,1)} %copy-done.6, bf16[4,1152,128]{2,1,0:T(8,128)(2,1)} %collective-permute-done.6.refs_1_, ...), custom_call_target="tpu_custom_call" | custom-call | flops 8000000000 | bytes 14000000 | tf_op jit(solution)/shard_map/experts/pallas_call | solution.py:482
  137.9 1.0 copy-done.23
  138.9 21.9 %experts.5 = (bf16[2048,896]{1,0:T(8,128)(2,1)}, bf16[4,1152,128]{2,1,0:T(8,128)(2,1)}, bf16[4,1152,128]{2,1,0:T(8,128)(2,1)}) custom-call(s32[80]{0:T(128)} %pad_add_fusion.2.table, bf16[4,1152,128]{2,1,0:T(8,128)(2,1)} %collective-permute-done.18.refs_0_, bf16[4,1152,128]{2,1,0:T(8,128)(2,1)} %copy-done.23, ...), custom_call_target="tpu_custom_call" | custom-call | flops 8000000000 | bytes 14000000 | tf_op jit(solution)/shard_map/experts/pallas_call | solution.py:482
  160.8 41.4 %experts.4 = (bf16[2048,896]{1,0:T(8,128)(2,1)}, bf16[4,1152,128]{2,1,0:T(8,128)(2,1)}, bf16[4,1152,128]{2,1,0:T(8,128)(2,1)}, bf16[4,1152,128]{2,1,0:T(8,128)(2,1)}, bf16[4,1152,128]{2,1,0:T(8,128)(2,1)}) custom-call(s32[80]{0:T(128)} %pad_add_fusion.2.table, bf16[4,1152,128]{2,1,0:T(8,128)(2,1)} %collective-permute-done.14.refs_0_, ...), custom_call_target="tpu_custom_call" | custom-call | flops 16000000000 | bytes 20000000 | tf_op jit(solution)/shard_map/experts/pallas_call | solution.py:482
  202.2 53.7 %attention_backward.1 = (bf16[2048,384]{1,0:T(8,128)(2,1)}, bf16[2048,384]{1,0:T(8,128)(2,1)}, bf16[32,160,128]{2,1,0:T(8,128)(2,1)}, f32[8,384]{1,0:T(8,128)}, f32[8,128]{1,0:T(8,128)}) custom-call(s32[32]{0:T(128)} %reshape.447.win, s32[2]{0:T(128)} %pad_add_fusion.1.place, bf16[2048,896]{1,0:T(8,128)(2,1)} %get-tuple-element.40.refs_0_, ...), custom_call_target="tpu_custom_call" | custom-call | flops 40000000000 | bytes 30000000 | tf_op jit(solution)/shard_map/attention_backward/pallas_call | solution.py:702
  257.8 2.0 collective-permute-start.40
  259.8 1.4 fusion.50
  261.4 1.4 collective-permute-start.43
  262.8 3.7 collective-permute-start.42
  266.5 1.6 collective-permute-done.42
  268.1 2.0 collective-permute-done.41
  270.6 1.6 collective-permute-start.45
  272.2 2.3 collective-permute-start.44
  276.3 1.4 fusion
  278.1 1.5 collective-permute-start.23
  279.5 1.8 collective-permute-start.22
  281.4 3.5 collective-permute-done.21
  284.9 2.4 collective-permute-done.23
  287.3 1.4 collective-permute-done.22
  288.9 2.0 collective-permute-start.26
  290.9 1.5 collective-permute-start.25
  293.4 1.4 collective-permute-done.26
  294.8 1.0 collective-permute-done.25
  297.1 1.7 collective-permute-start.29
  300.4 1.5 collective-permute-start.33
  302.0 1.0 pad_maximum_fusion.7
  303.0 23.1 %collective-permute-done.29 = bf16[4,1152,128]{2,1,0:T(8,128)(2,1)S(1)} collective-permute-done((bf16[4,1152,128]{2,1,0:T(8,128)(2,1)S(1)}, bf16[4,1152,128]{2,1,0:T(8,128)(2,1)S(1)}, u32[]{:S(2)}, u32[]{:S(2)}) %collective-permute-start.29) | collective-permute-done | bytes 1179680 | tf_op jit(solution)/shard_map/ppermute | solution.py:748
  326.1 25.6 %collective-permute-done.31 = bf16[4,1152,128]{2,1,0:T(8,128)(2,1)S(1)} collective-permute-done((bf16[4,1152,128]{2,1,0:T(8,128)(2,1)S(1)}, bf16[4,1152,128]{2,1,0:T(8,128)(2,1)S(1)}, u32[]{:S(2)}, u32[]{:S(2)}) %collective-permute-start.31) | collective-permute-done | bytes 1179680 | tf_op jit(solution)/shard_map/ppermute | solution.py:748
  352.8 2.0 collective-permute-start.39
  354.8 2.5 collective-permute-start.37
  358.1 1.9 collective-permute-start.36
  360.4 1.2 collective-permute-start.35
  361.6 2.5 collective-permute-done.38
  366.4 1.2 pad_maximum_fusion.4
  367.6 1.1 copy.68
  368.7 3.8 collective-permute-done.36
  372.5 6.8 %collective-permute-done.35 = bf16[2,384,128]{2,1,0:T(8,128)(2,1)} collective-permute-done((bf16[2,384,128]{2,1,0:T(8,128)(2,1)}, bf16[2,384,128]{2,1,0:T(8,128)(2,1)}, u32[]{:S(2)}, u32[]{:S(2)}) %collective-permute-start.35) | collective-permute-done | bytes 196640 | tf_op jit(solution)/shard_map/ppermute | solution.py:748
  379.3 2.2 fusion.43
  381.5 1.3 pad_maximum_fusion
  (199 shorter events, 24.2 us)
Async XLA Ops:
  0.6 13.5 %copy-start.10 = (f32[4,1,128,384]{3,2,1,0:T(8,128)S(1)}, f32[4,1,128,384]{3,2,1,0:T(8,128)}, u32[]{:S(2)}) copy-start(f32[4,1,128,384]{3,2,1,0:T(8,128)} %param.20) | copy-start | bytes 2359300
  3.6 11.8 %copy-start.15 = (s32[2,1024]{1,0:T(2,128)S(1)}, s32[2,1024]{1,0:T(2,128)}, u32[]{:S(2)}) copy-start(s32[2,1024]{1,0:T(2,128)} %param.14) | copy-start | bytes 24580
  3.6 14.0 %copy-start.17 = (s32[2048,2]{0,1:T(2,128)S(1)}, s32[2048,2]{0,1:T(2,128)}, u32[]{:S(2)}) copy-start(s32[2048,2]{0,1:T(2,128)} %param.13) | copy-start | bytes 49156
  3.6 19.2 %collective-permute-start.9 = (bf16[1,160,128]{2,1,0:T(8,128)(2,1)S(1)}, bf16[1,160,128]{2,1,0:T(8,128)(2,1)S(1)}, u32[]{:S(2)}, u32[]{:S(2)}) collective-permute-start(bf16[1,160,128]{2,1,0:T(8,128)(2,1)S(1)} %pad_bitcast_fusion), channel_id=1, source_target_pairs={{0,3},{1,2},{2,1},{3,0},{4,7},{5,6},{6,5},{7,4},{8,11},{9,10},{10,... | collective-permute-start | bytes 122888 | tf_op jit(solution)/shard_map/ppermute | solution.py:748
  8.7 14.6 %collective-permute-start.8 = (bf16[1,160,128]{2,1,0:T(8,128)(2,1)S(1)}, bf16[1,160,128]{2,1,0:T(8,128)(2,1)}, u32[]{:S(2)}, u32[]{:S(2)}) collective-permute-start(bf16[1,160,128]{2,1,0:T(8,128)(2,1)S(1)} %pad_bitcast_fusion), channel_id=1, source_target_pairs={{0,2},{1,3},{2,0},{3,1},{4,6},{5,7},{6,4},{7,5},{8,10},{9,11},{10,... | collective-permute-start | bytes 122888 | tf_op jit(solution)/shard_map/ppermute | solution.py:748
  8.7 18.5 %collective-permute-start.7 = (bf16[1,160,128]{2,1,0:T(8,128)(2,1)S(1)}, bf16[1,160,128]{2,1,0:T(8,128)(2,1)}, u32[]{:S(2)}, u32[]{:S(2)}) collective-permute-start(bf16[1,160,128]{2,1,0:T(8,128)(2,1)S(1)} %pad_bitcast_fusion), channel_id=1, source_target_pairs={{0,1},{1,0},{2,3},{3,2},{4,5},{5,4},{6,7},{7,6},{8,9},{9,8},{10,11... | collective-permute-start | bytes 122888 | tf_op jit(solution)/shard_map/ppermute | solution.py:748
  10.4 32.0 %collective-permute-start.2 = (bf16[2,384,128]{2,1,0:T(8,128)(2,1)S(1)}, bf16[2,384,128]{2,1,0:T(8,128)(2,1)S(1)}, u32[]{:S(2)}, u32[]{:S(2)}) collective-permute-start(bf16[2,384,128]{2,1,0:T(8,128)(2,1)S(1)} %bitcast_convert_fusion), channel_id=1, source_target_pairs={{0,3},{1,2},{2,1},{3,0},{4,7},{5,6},{6,5},{7,4},{8,11},{9,10},{10,... | collective-permute-start | bytes 589832 | tf_op jit(solution)/shard_map/ppermute | solution.py:748
  15.1 12.1 %collective-permute-start.5 = (bf16[128,384]{0,1:T(8,128)(2,1)S(1)}, bf16[128,384]{0,1:T(8,128)(2,1)S(1)}, u32[]{:S(2)}, u32[]{:S(2)}) collective-permute-start(bf16[128,384]{0,1:T(8,128)(2,1)S(1)} %bitcast_convert_fusion.1), channel_id=1, source_target_pairs={{0,3},{1,2},{2,1},{3,0},{4,7},{5,6},{6,5},{7,4},{8,11},{9,10},{10,... | collective-permute-start | bytes 294920 | tf_op jit(solution)/shard_map/ppermute | solution.py:748
  22.8 20.1 %collective-permute-start.1 = (bf16[2,384,128]{2,1,0:T(8,128)(2,1)S(1)}, bf16[2,384,128]{2,1,0:T(8,128)(2,1)S(1)}, u32[]{:S(2)}, u32[]{:S(2)}) collective-permute-start(bf16[2,384,128]{2,1,0:T(8,128)(2,1)S(1)} %bitcast_convert_fusion), channel_id=1, source_target_pairs={{0,2},{1,3},{2,0},{3,1},{4,6},{5,7},{6,4},{7,5},{8,10},{9,11},{10,... | collective-permute-start | bytes 589832 | tf_op jit(solution)/shard_map/ppermute | solution.py:748
  23.3 19.6 %collective-permute-start = (bf16[2,384,128]{2,1,0:T(8,128)(2,1)S(1)}, bf16[2,384,128]{2,1,0:T(8,128)(2,1)S(1)}, u32[]{:S(2)}, u32[]{:S(2)}) collective-permute-start(bf16[2,384,128]{2,1,0:T(8,128)(2,1)S(1)} %bitcast_convert_fusion), channel_id=1, source_target_pairs={{0,1},{1,0},{2,3},{3,2},{4,5},{5,4},{6,7},{7,6},{8,9},{9,8},{10,11... | collective-permute-start | bytes 589832 | tf_op jit(solution)/shard_map/ppermute | solution.py:748
  27.2 11.7 %collective-permute-start.4 = (bf16[128,384]{0,1:T(8,128)(2,1)S(1)}, bf16[128,384]{0,1:T(8,128)(2,1)S(1)}, u32[]{:S(2)}, u32[]{:S(2)}) collective-permute-start(bf16[128,384]{0,1:T(8,128)(2,1)S(1)} %bitcast_convert_fusion.1), channel_id=1, source_target_pairs={{0,2},{1,3},{2,0},{3,1},{4,6},{5,7},{6,4},{7,5},{8,10},{9,11},{10,... | collective-permute-start | bytes 294920 | tf_op jit(solution)/shard_map/ppermute | solution.py:748
  27.3 13.2 %collective-permute-start.3 = (bf16[128,384]{0,1:T(8,128)(2,1)S(1)}, bf16[128,384]{0,1:T(8,128)(2,1)S(1)}, u32[]{:S(2)}, u32[]{:S(2)}) collective-permute-start(bf16[128,384]{0,1:T(8,128)(2,1)S(1)} %bitcast_convert_fusion.1), channel_id=1, source_target_pairs={{0,1},{1,0},{2,3},{3,2},{4,5},{5,4},{6,7},{7,6},{8,9},{9,8},{10,11... | collective-permute-start | bytes 294920 | tf_op jit(solution)/shard_map/ppermute | solution.py:748
  38.9 7.1 %collective-permute-start.11 = (bf16[4,160,128]{2,1,0:T(8,128)(2,1)}, bf16[4,160,128]{2,1,0:T(8,128)(2,1)}, u32[]{:S(2)}, u32[]{:S(2)}) collective-permute-start(bf16[4,160,128]{2,1,0:T(8,128)(2,1)} %get-tuple-element.139), channel_id=1, source_target_pairs={{0,16},{4,20},{8,24},{12,28},{16,0},{20,4},{24,8},{28,12},{1,17},{... | collective-permute-start | bytes 491528 | tf_op jit(solution)/shard_map/ppermute | solution.py:748
  40.4 7.5 %collective-permute-start.10 = (bf16[4,160,128]{2,1,0:T(8,128)(2,1)}, bf16[4,160,128]{2,1,0:T(8,128)(2,1)}, u32[]{:S(2)}, u32[]{:S(2)}) collective-permute-start(bf16[4,160,128]{2,1,0:T(8,128)(2,1)} %get-tuple-element.139), channel_id=1, source_target_pairs={{0,8},{4,12},{8,0},{12,4},{16,24},{20,28},{24,16},{28,20},{1,9},{5... | collective-permute-start | bytes 491528 | tf_op jit(solution)/shard_map/ppermute | solution.py:748
  42.4 8.4 %collective-permute-start.12 = (bf16[4,160,128]{2,1,0:T(8,128)(2,1)}, bf16[4,160,128]{2,1,0:T(8,128)(2,1)}, u32[]{:S(2)}, u32[]{:S(2)}) collective-permute-start(bf16[4,160,128]{2,1,0:T(8,128)(2,1)} %get-tuple-element.139), channel_id=1, source_target_pairs={{0,24},{4,28},{8,16},{12,20},{16,8},{20,12},{24,0},{28,4},{1,25},{... | collective-permute-start | bytes 491528 | tf_op jit(solution)/shard_map/ppermute | solution.py:748
  43.4 23.5 %copy-start.6 = (bf16[4,1152,128]{2,1,0:T(8,128)(2,1)}, bf16[4,1152,128]{2,1,0:T(8,128)(2,1)S(1)}, u32[]{:S(2)}) copy-start(bf16[4,1152,128]{2,1,0:T(8,128)(2,1)S(1)} %pad_maximum_fusion.2.refs_0_) | copy-start | bytes 3538948
  43.4 32.7 %collective-permute-start.18 = (bf16[4,1152,128]{2,1,0:T(8,128)(2,1)S(1)}, bf16[4,1152,128]{2,1,0:T(8,128)(2,1)}, u32[]{:S(2)}, u32[]{:S(2)}) collective-permute-start(bf16[4,1152,128]{2,1,0:T(8,128)(2,1)S(1)} %pad_maximum_fusion.2.refs_0_), channel_id=1, source_target_pairs={{0,24},{4,28},{8,16},{12,20},{16,8},{20,12},{24,0},{28,4},{1,25},{... | collective-permute-start | bytes 3538952 | tf_op jit(solution)/shard_map/ppermute | solution.py:748
  52.8 14.1 %collective-permute-start.13 = (bf16[4,4,160,128]{3,2,1,0:T(8,128)(2,1)}, bf16[4,4,160,128]{3,2,1,0:T(8,128)(2,1)}, u32[]{:S(2)}, u32[]{:S(2)}) collective-permute-start(bf16[4,4,160,128]{3,2,1,0:T(8,128)(2,1)} %get-tuple-element.130), channel_id=1, source_target_pairs={{0,4},{4,0},{8,12},{12,8},{16,20},{20,16},{24,28},{28,24},{1,5},{5... | collective-permute-start | bytes 1966088 | tf_op jit(solution)/shard_map/ppermute | solution.py:748
  63.3 47.7 %collective-permute-start.16 = (bf16[4,1152,128]{2,1,0:T(8,128)(2,1)S(1)}, bf16[4,1152,128]{2,1,0:T(8,128)(2,1)S(1)}, u32[]{:S(2)}, u32[]{:S(2)}) collective-permute-start(bf16[4,1152,128]{2,1,0:T(8,128)(2,1)S(1)} %pad_maximum_fusion.2.refs_0_), channel_id=1, source_target_pairs={{0,16},{4,20},{8,24},{12,28},{16,0},{20,4},{24,8},{28,12},{1,17},{... | collective-permute-start | bytes 3538952 | tf_op jit(solution)/shard_map/ppermute | solution.py:748
  65.4 47.3 %collective-permute-start.14 = (bf16[4,1152,128]{2,1,0:T(8,128)(2,1)S(1)}, bf16[4,1152,128]{2,1,0:T(8,128)(2,1)}, u32[]{:S(2)}, u32[]{:S(2)}) collective-permute-start(bf16[4,1152,128]{2,1,0:T(8,128)(2,1)S(1)} %pad_maximum_fusion.2.refs_0_), channel_id=1, source_target_pairs={{0,8},{4,12},{8,0},{12,4},{16,24},{20,28},{24,16},{28,20},{1,9},{5... | collective-permute-start | bytes 3538952 | tf_op jit(solution)/shard_map/ppermute | solution.py:748
  66.9 45.9 %collective-permute-start.6 = (bf16[4,1152,128]{2,1,0:T(8,128)(2,1)S(1)}, bf16[4,1152,128]{2,1,0:T(8,128)(2,1)}, u32[]{:S(2)}, u32[]{:S(2)}) collective-permute-start(bf16[4,1152,128]{2,1,0:T(8,128)(2,1)S(1)} %pad_maximum_fusion.2.refs_0_), channel_id=1, source_target_pairs={{0,4},{4,0},{8,12},{12,8},{16,20},{20,16},{24,28},{28,24},{1,5},{5... | collective-permute-start | bytes 3538952 | tf_op jit(solution)/shard_map/ppermute | solution.py:748
  76.1 61.8 %collective-permute-start.19 = (bf16[4,1152,128]{2,1,0:T(8,128)(2,1)}, bf16[4,1152,128]{2,1,0:T(8,128)(2,1)S(1)}, u32[]{:S(2)}, u32[]{:S(2)}) collective-permute-start(bf16[4,1152,128]{2,1,0:T(8,128)(2,1)} %collective-permute-done.18.refs_0_), channel_id=1, source_target_pairs={{0,4},{4,0},{8,12},{12,8},{16,20},{20,16},{24,28},{28,24},{1,5},{5... | collective-permute-start | bytes 3538952 | tf_op jit(solution)/shard_map/ppermute | solution.py:748
  111.1 26.9 %copy-start.22 = (bf16[4,1152,128]{2,1,0:T(8,128)(2,1)}, bf16[4,1152,128]{2,1,0:T(8,128)(2,1)S(1)}, u32[]{:S(2)}) copy-start(bf16[4,1152,128]{2,1,0:T(8,128)(2,1)S(1)} %collective-permute-done.16.refs_2_) | copy-start | bytes 3538948
  111.1 49.8 %collective-permute-start.17 = (bf16[4,1152,128]{2,1,0:T(8,128)(2,1)S(1)}, bf16[4,1152,128]{2,1,0:T(8,128)(2,1)}, u32[]{:S(2)}, u32[]{:S(2)}) collective-permute-start(bf16[4,1152,128]{2,1,0:T(8,128)(2,1)S(1)} %collective-permute-done.16.refs_2_), channel_id=1, source_target_pairs={{0,4},{4,0},{8,12},{12,8},{16,20},{20,16},{24,28},{28,24},{1,5},{5... | collective-permute-start | bytes 3538952 | tf_op jit(solution)/shard_map/ppermute | solution.py:748
  112.7 48.2 %collective-permute-start.15 = (bf16[4,1152,128]{2,1,0:T(8,128)(2,1)}, bf16[4,1152,128]{2,1,0:T(8,128)(2,1)}, u32[]{:S(2)}, u32[]{:S(2)}) collective-permute-start(bf16[4,1152,128]{2,1,0:T(8,128)(2,1)} %collective-permute-done.14.refs_0_), channel_id=1, source_target_pairs={{0,4},{4,0},{8,12},{12,8},{16,20},{20,16},{24,28},{28,24},{1,5},{5... | collective-permute-start | bytes 3538952 | tf_op jit(solution)/shard_map/ppermute | solution.py:748
  255.9 18.6 %copy-start.16 = (f32[4,780]{1,0:T(4,128)S(1)}, f32[4,780]{1,0:T(4,128)}, u32[]{:S(2)}) copy-start(f32[4,780]{1,0:T(4,128)} %param.21) | copy-start | bytes 37444
  255.9 19.3 %copy-start.9 = (f32[1,1,128,384]{3,2,1,0:T(8,128)S(1)}, f32[1,1,128,384]{3,2,1,0:T(8,128)}, u32[]{:S(2)}) copy-start(f32[1,1,128,384]{3,2,1,0:T(8,128)} %get-tuple-element.119) | copy-start | bytes 589828
  256.0 19.4 %copy-start.8 = (f32[1,1,128,384]{3,2,1,0:T(8,128)S(1)}, f32[1,1,128,384]{3,2,1,0:T(8,128)}, u32[]{:S(2)}) copy-start(f32[1,1,128,384]{3,2,1,0:T(8,128)} %get-tuple-element.120) | copy-start | bytes 589828
  257.8 3.5 collective-permute-start.40
  259.8 15.7 %copy-start.7 = (f32[1,1,128,384]{3,2,1,0:T(8,128)S(1)}, f32[1,1,128,384]{3,2,1,0:T(8,128)}, u32[]{:S(2)}) copy-start(f32[1,1,128,384]{3,2,1,0:T(8,128)} %get-tuple-element.121) | copy-start | bytes 589828
  261.2 15.0 %collective-permute-start.20 = (bf16[4,4,160,128]{3,2,1,0:T(8,128)(2,1)S(1)}, bf16[4,4,160,128]{3,2,1,0:T(8,128)(2,1)}, u32[]{:S(2)}, u32[]{:S(2)}) collective-permute-start(bf16[4,4,160,128]{3,2,1,0:T(8,128)(2,1)S(1)} %bitcast.224), channel_id=1, source_target_pairs={{0,4},{4,0},{8,12},{12,8},{16,20},{20,16},{24,28},{28,24},{1,5},{5... | collective-permute-start | bytes 1966088 | tf_op jit(solution)/shard_map/ppermute | solution.py:748
  261.4 5.1 %collective-permute-start.43 = (f32[8,128]{1,0:T(8,128)S(1)}, f32[8,128]{1,0:T(8,128)S(1)}, u32[]{:S(2)}, u32[]{:S(2)}) collective-permute-start(f32[8,128]{1,0:T(8,128)S(1)} %fusion.55), channel_id=1, source_target_pairs={{0,24},{4,28},{8,16},{12,20},{16,8},{20,12},{24,0},{28,4},{1,25},{... | collective-permute-start | bytes 12296 | tf_op jit(solution)/shard_map/ppermute | solution.py:748
  262.8 5.3 %collective-permute-start.42 = (f32[8,128]{1,0:T(8,128)S(1)}, f32[8,128]{1,0:T(8,128)S(1)}, u32[]{:S(2)}, u32[]{:S(2)}) collective-permute-start(f32[8,128]{1,0:T(8,128)S(1)} %fusion.55), channel_id=1, source_target_pairs={{0,16},{4,20},{8,24},{12,28},{16,0},{20,4},{24,8},{28,12},{1,17},{... | collective-permute-start | bytes 12296 | tf_op jit(solution)/shard_map/ppermute | solution.py:748
  266.5 3.6 collective-permute-start.41
  270.1 5.6 %collective-permute-start.46 = (f32[8,128]{1,0:T(8,128)S(1)}, f32[8,128]{1,0:T(8,128)S(1)}, u32[]{:S(2)}, u32[]{:S(2)}) collective-permute-start(f32[8,128]{1,0:T(8,128)S(1)} %add_add_fusion), channel_id=1, source_target_pairs={{0,3},{1,2},{2,1},{3,0},{4,7},{5,6},{6,5},{7,4},{8,11},{9,10},{10,... | collective-permute-start | bytes 12296 | tf_op jit(solution)/shard_map/ppermute | solution.py:748
  270.6 5.7 %collective-permute-start.45 = (f32[8,128]{1,0:T(8,128)S(1)}, f32[8,128]{1,0:T(8,128)S(1)}, u32[]{:S(2)}, u32[]{:S(2)}) collective-permute-start(f32[8,128]{1,0:T(8,128)S(1)} %add_add_fusion), channel_id=1, source_target_pairs={{0,2},{1,3},{2,0},{3,1},{4,6},{5,7},{6,4},{7,5},{8,10},{9,11},{10,... | collective-permute-start | bytes 12296 | tf_op jit(solution)/shard_map/ppermute | solution.py:748
  272.2 4.1 %collective-permute-start.44 = (f32[8,128]{1,0:T(8,128)S(1)}, f32[8,128]{1,0:T(8,128)S(1)}, u32[]{:S(2)}, u32[]{:S(2)}) collective-permute-start(f32[8,128]{1,0:T(8,128)S(1)} %add_add_fusion), channel_id=1, source_target_pairs={{0,1},{1,0},{2,3},{3,2},{4,5},{5,4},{6,7},{7,6},{8,9},{9,8},{10,11... | collective-permute-start | bytes 12296 | tf_op jit(solution)/shard_map/ppermute | solution.py:748
  275.7 27.3 %collective-permute-start.27 = (bf16[4,1152,128]{2,1,0:T(8,128)(2,1)}, bf16[4,1152,128]{2,1,0:T(8,128)(2,1)S(1)}, u32[]{:S(2)}, u32[]{:S(2)}) collective-permute-start(bf16[4,1152,128]{2,1,0:T(8,128)(2,1)} %get-tuple-element.54), channel_id=1, source_target_pairs={{0,4},{4,0},{8,12},{12,8},{16,20},{20,16},{24,28},{28,24},{1,5},{5... | collective-permute-start | bytes 3538952 | tf_op jit(solution)/shard_map/ppermute | solution.py:748
  275.8 21.0 %collective-permute-start.28 = (bf16[4,1152,128]{2,1,0:T(8,128)(2,1)}, bf16[4,1152,128]{2,1,0:T(8,128)(2,1)S(1)}, u32[]{:S(2)}, u32[]{:S(2)}) collective-permute-start(bf16[4,1152,128]{2,1,0:T(8,128)(2,1)} %get-tuple-element.56), channel_id=1, source_target_pairs={{0,4},{4,0},{8,12},{12,8},{16,20},{20,16},{24,28},{28,24},{1,5},{5... | collective-permute-start | bytes 3538952 | tf_op jit(solution)/shard_map/ppermute | solution.py:748
  276.3 17.1 %copy-start.21 = (bf16[4,1152,128]{2,1,0:T(8,128)(2,1)S(1)}, bf16[4,1152,128]{2,1,0:T(8,128)(2,1)}, u32[]{:S(2)}) copy-start(bf16[4,1152,128]{2,1,0:T(8,128)(2,1)} %get-tuple-element.58) | copy-start | bytes 3538948
  277.7 17.1 %copy-start.20 = (bf16[4,1152,128]{2,1,0:T(8,128)(2,1)S(1)}, bf16[4,1152,128]{2,1,0:T(8,128)(2,1)}, u32[]{:S(2)}) copy-start(bf16[4,1152,128]{2,1,0:T(8,128)(2,1)} %get-tuple-element.60) | copy-start | bytes 3538948
  277.7 18.1 %copy-start.13 = (f32[18528]{0:T(1024)S(1)}, f32[18528]{0:T(1024)}, u32[]{:S(2)}) copy-start(f32[18528]{0:T(1024)} %get-tuple-element.83) | copy-start | bytes 222340
  277.7 18.1 %copy-start.14 = (f32[18528]{0:T(1024)S(1)}, f32[18528]{0:T(1024)}, u32[]{:S(2)}) copy-start(f32[18528]{0:T(1024)} %get-tuple-element.84) | copy-start | bytes 222340
  277.7 18.9 %copy-start.12 = (f32[18528]{0:T(1024)S(1)}, f32[18528]{0:T(1024)}, u32[]{:S(2)}) copy-start(f32[18528]{0:T(1024)} %get-tuple-element.86) | copy-start | bytes 222340
  277.7 19.1 %copy-start.5 = (bf16[4,1152,128]{2,1,0:T(8,128)(2,1)S(1)}, bf16[4,1152,128]{2,1,0:T(8,128)(2,1)}, u32[]{:S(2)}) copy-start(bf16[4,1152,128]{2,1,0:T(8,128)(2,1)} %get-tuple-element.55) | copy-start | bytes 3538948
  277.7 7.1 %collective-permute-start.21 = (bf16[4,160,128]{2,1,0:T(8,128)(2,1)S(1)}, bf16[4,160,128]{2,1,0:T(8,128)(2,1)S(1)}, u32[]{:S(2)}, u32[]{:S(2)}) collective-permute-start(bf16[4,160,128]{2,1,0:T(8,128)(2,1)S(1)} %get-tuple-element.126), channel_id=1, source_target_pairs={{0,8},{4,12},{8,0},{12,4},{16,24},{20,28},{24,16},{28,20},{1,9},{5... | collective-permute-start | bytes 491528 | tf_op jit(solution)/shard_map/ppermute | solution.py:748
  278.1 9.2 %collective-permute-start.23 = (bf16[4,160,128]{2,1,0:T(8,128)(2,1)S(1)}, bf16[4,160,128]{2,1,0:T(8,128)(2,1)S(1)}, u32[]{:S(2)}, u32[]{:S(2)}) collective-permute-start(bf16[4,160,128]{2,1,0:T(8,128)(2,1)S(1)} %get-tuple-element.127), channel_id=1, source_target_pairs={{0,24},{4,28},{8,16},{12,20},{16,8},{20,12},{24,0},{28,4},{1,25},{... | collective-permute-start | bytes 491528 | tf_op jit(solution)/shard_map/ppermute | solution.py:748
  279.5 9.2 %collective-permute-start.22 = (bf16[4,160,128]{2,1,0:T(8,128)(2,1)S(1)}, bf16[4,160,128]{2,1,0:T(8,128)(2,1)S(1)}, u32[]{:S(2)}, u32[]{:S(2)}) collective-permute-start(bf16[4,160,128]{2,1,0:T(8,128)(2,1)S(1)} %get-tuple-element.128), channel_id=1, source_target_pairs={{0,16},{4,20},{8,24},{12,28},{16,0},{20,4},{24,8},{28,12},{1,17},{... | collective-permute-start | bytes 491528 | tf_op jit(solution)/shard_map/ppermute | solution.py:748
  288.8 4.6 %collective-permute-start.24 = (bf16[160,128]{1,0:T(8,128)(2,1)S(1)}, bf16[160,128]{1,0:T(8,128)(2,1)S(1)}, u32[]{:S(2)}, u32[]{:S(2)}) collective-permute-start(bf16[160,128]{1,0:T(8,128)(2,1)S(1)} %get-tuple-element.135), channel_id=1, source_target_pairs={{0,1},{1,0},{2,3},{3,2},{4,5},{5,4},{6,7},{7,6},{8,9},{9,8},{10,11... | collective-permute-start | bytes 122888 | tf_op jit(solution)/shard_map/ppermute | solution.py:748
  288.9 5.9 %collective-permute-start.26 = (bf16[160,128]{1,0:T(8,128)(2,1)S(1)}, bf16[160,128]{1,0:T(8,128)(2,1)S(1)}, u32[]{:S(2)}, u32[]{:S(2)}) collective-permute-start(bf16[160,128]{1,0:T(8,128)(2,1)S(1)} %get-tuple-element.136), channel_id=1, source_target_pairs={{0,3},{1,2},{2,1},{3,0},{4,7},{5,6},{6,5},{7,4},{8,11},{9,10},{10,... | collective-permute-start | bytes 122888 | tf_op jit(solution)/shard_map/ppermute | solution.py:748
  290.9 4.9 %collective-permute-start.25 = (bf16[160,128]{1,0:T(8,128)(2,1)S(1)}, bf16[160,128]{1,0:T(8,128)(2,1)S(1)}, u32[]{:S(2)}, u32[]{:S(2)}) collective-permute-start(bf16[160,128]{1,0:T(8,128)(2,1)S(1)} %get-tuple-element.137), channel_id=1, source_target_pairs={{0,2},{1,3},{2,0},{3,1},{4,6},{5,7},{6,4},{7,5},{8,10},{9,11},{10,... | collective-permute-start | bytes 122888 | tf_op jit(solution)/shard_map/ppermute | solution.py:748
  293.4 5.5 %collective-permute-start.30 = (bf16[4,1152,128]{2,1,0:T(8,128)(2,1)S(1)}, bf16[4,1152,128]{2,1,0:T(8,128)(2,1)S(1)}, u32[]{:S(2)}, u32[]{:S(2)}) collective-permute-start(bf16[4,1152,128]{2,1,0:T(8,128)(2,1)S(1)} %copy-done.21), channel_id=1, source_target_pairs={{0,4},{4,0},{8,12},{12,8},{16,20},{20,16},{24,28},{28,24},{1,5},{5... | collective-permute-start | bytes 3538952 | tf_op jit(solution)/shard_map/ppermute | solution.py:748
  294.8 5.3 %collective-permute-start.32 = (bf16[4,1152,128]{2,1,0:T(8,128)(2,1)S(1)}, bf16[4,1152,128]{2,1,0:T(8,128)(2,1)S(1)}, u32[]{:S(2)}, u32[]{:S(2)}) collective-permute-start(bf16[4,1152,128]{2,1,0:T(8,128)(2,1)S(1)} %copy-done.20), channel_id=1, source_target_pairs={{0,4},{4,0},{8,12},{12,8},{16,20},{20,16},{24,28},{28,24},{1,5},{5... | collective-permute-start | bytes 3538952 | tf_op jit(solution)/shard_map/ppermute | solution.py:748
  297.1 29.0 %collective-permute-start.29 = (bf16[4,1152,128]{2,1,0:T(8,128)(2,1)S(1)}, bf16[4,1152,128]{2,1,0:T(8,128)(2,1)S(1)}, u32[]{:S(2)}, u32[]{:S(2)}) collective-permute-start(bf16[4,1152,128]{2,1,0:T(8,128)(2,1)S(1)} %add_convert_fusion.3), channel_id=1, source_target_pairs={{0,8},{4,12},{8,0},{12,4},{16,24},{20,28},{24,16},{28,20},{1,9},{5... | collective-permute-start | bytes 3538952 | tf_op jit(solution)/shard_map/ppermute | solution.py:748
  299.2 52.5 %collective-permute-start.31 = (bf16[4,1152,128]{2,1,0:T(8,128)(2,1)S(1)}, bf16[4,1152,128]{2,1,0:T(8,128)(2,1)S(1)}, u32[]{:S(2)}, u32[]{:S(2)}) collective-permute-start(bf16[4,1152,128]{2,1,0:T(8,128)(2,1)S(1)} %add_convert_fusion.2), channel_id=1, source_target_pairs={{0,16},{4,20},{8,24},{12,28},{16,0},{20,4},{24,8},{28,12},{1,17},{... | collective-permute-start | bytes 3538952 | tf_op jit(solution)/shard_map/ppermute | solution.py:748
  300.1 51.5 %copy-start.2 = (bf16[4,1152,128]{2,1,0:T(8,128)(2,1)S(1)}, bf16[4,1152,128]{2,1,0:T(8,128)(2,1)}, u32[]{:S(2)}) copy-start(bf16[4,1152,128]{2,1,0:T(8,128)(2,1)} %get-tuple-element.53) | copy-start | bytes 3538948
  300.4 51.2 %collective-permute-start.33 = (bf16[4,1152,128]{2,1,0:T(8,128)(2,1)S(1)}, bf16[4,1152,128]{2,1,0:T(8,128)(2,1)S(1)}, u32[]{:S(2)}, u32[]{:S(2)}) collective-permute-start(bf16[4,1152,128]{2,1,0:T(8,128)(2,1)S(1)} %add_convert_fusion.1), channel_id=1, source_target_pairs={{0,24},{4,28},{8,16},{12,20},{16,8},{20,12},{24,0},{28,4},{1,25},{... | collective-permute-start | bytes 3538952 | tf_op jit(solution)/shard_map/ppermute | solution.py:748
  352.8 7.6 %collective-permute-start.39 = (bf16[128,384]{0,1:T(8,128)(2,1)S(1)}, bf16[128,384]{0,1:T(8,128)(2,1)S(1)}, u32[]{:S(2)}, u32[]{:S(2)}) collective-permute-start(bf16[128,384]{0,1:T(8,128)(2,1)S(1)} %bitcast.227), channel_id=1, source_target_pairs={{0,3},{1,2},{2,1},{3,0},{4,7},{5,6},{6,5},{7,4},{8,11},{9,10},{10,... | collective-permute-start | bytes 294920 | tf_op jit(solution)/shard_map/ppermute | solution.py:748
  354.8 9.3 %collective-permute-start.38 = (bf16[128,384]{0,1:T(8,128)(2,1)S(1)}, bf16[128,384]{0,1:T(8,128)(2,1)S(1)}, u32[]{:S(2)}, u32[]{:S(2)}) collective-permute-start(bf16[128,384]{0,1:T(8,128)(2,1)S(1)} %bitcast.226), channel_id=1, source_target_pairs={{0,2},{1,3},{2,0},{3,1},{4,6},{5,7},{6,4},{7,5},{8,10},{9,11},{10,... | collective-permute-start | bytes 294920 | tf_op jit(solution)/shard_map/ppermute | solution.py:748
  354.8 9.3 %collective-permute-start.37 = (bf16[128,384]{0,1:T(8,128)(2,1)S(1)}, bf16[128,384]{0,1:T(8,128)(2,1)S(1)}, u32[]{:S(2)}, u32[]{:S(2)}) collective-permute-start(bf16[128,384]{0,1:T(8,128)(2,1)S(1)} %bitcast.225), channel_id=1, source_target_pairs={{0,1},{1,0},{2,3},{3,2},{4,5},{5,4},{6,7},{7,6},{8,9},{9,8},{10,11... | collective-permute-start | bytes 294920 | tf_op jit(solution)/shard_map/ppermute | solution.py:748
  358.1 10.7 %collective-permute-start.34 = (bf16[2,384,128]{2,1,0:T(8,128)(2,1)}, bf16[2,384,128]{2,1,0:T(8,128)(2,1)}, u32[]{:S(2)}, u32[]{:S(2)}) collective-permute-start(bf16[2,384,128]{2,1,0:T(8,128)(2,1)} %get-tuple-element.123), channel_id=1, source_target_pairs={{0,1},{1,0},{2,3},{3,2},{4,5},{5,4},{6,7},{7,6},{8,9},{9,8},{10,11... | collective-permute-start | bytes 589832 | tf_op jit(solution)/shard_map/ppermute | solution.py:748
  358.1 14.4 %collective-permute-start.36 = (bf16[2,384,128]{2,1,0:T(8,128)(2,1)}, bf16[2,384,128]{2,1,0:T(8,128)(2,1)}, u32[]{:S(2)}, u32[]{:S(2)}) collective-permute-start(bf16[2,384,128]{2,1,0:T(8,128)(2,1)} %get-tuple-element.124), channel_id=1, source_target_pairs={{0,3},{1,2},{2,1},{3,0},{4,7},{5,6},{6,5},{7,4},{8,11},{9,10},{10,... | collective-permute-start | bytes 589832 | tf_op jit(solution)/shard_map/ppermute | solution.py:748
  360.4 18.9 %collective-permute-start.35 = (bf16[2,384,128]{2,1,0:T(8,128)(2,1)}, bf16[2,384,128]{2,1,0:T(8,128)(2,1)}, u32[]{:S(2)}, u32[]{:S(2)}) collective-permute-start(bf16[2,384,128]{2,1,0:T(8,128)(2,1)} %get-tuple-element.125), channel_id=1, source_target_pairs={{0,2},{1,3},{2,0},{3,1},{4,6},{5,7},{6,4},{7,5},{8,10},{9,11},{10,... | collective-permute-start | bytes 589832 | tf_op jit(solution)/shard_map/ppermute | solution.py:748
  366.4 12.9 %copy-start.1 = (f32[4,1,2,384,128]{4,3,2,1,0:T(8,128)S(1)}, f32[4,1,2,384,128]{4,3,2,1,0:T(8,128)}, u32[]{:S(2)}) copy-start(f32[4,1,2,384,128]{4,3,2,1,0:T(8,128)} %param.19) | copy-start | bytes 4718596
  (7 other events, 20.7 us)
